TPU v7x, 256 devices: a whole 4x4x8 slice. The times are simulated.
256 devices in a mesh: tm: 128 (over y, x, z), rhs: 2 (over core).
Axes of the slice: x: 4, y: 4, z: 8, core: 2. Of those that a mesh axis runs over, the one named last changes fastest.
Arguments:
- diag_blocks: float32 [512, 384, 384], P('tm')
- couplings: float32 [512, 384, 384], P('tm'), as said below
- arrow_coupling: float32 [512, 256, 384], P('tm', 'rhs')
- right_sides: float32 [512, 384, 128], P('tm', None, 'rhs')
- arrow_block: float32 [256, 256], P('rhs'), may hold values from -6 to 6
- arrow_rhs: float32 [256, 128], P(None, 'rhs'), may hold values from -6 to 6
Outputs:
- block_results: float32 [512, 384, 384], P('tm')
- coupling_results: float32 [512, 384, 384], P('tm')
- arrow_results: float32 [512, 256, 384], P('tm', 'rhs')
- rhs_results: float32 [512, 384, 128], P('tm', None, 'rhs')
- reduced_arrow: float32 [256, 256], P('rhs')
- reduced_arrow_rhs: float32 [256, 128], P(None, 'rhs')
Inputs may be any that keep to these rules, and one draw needn't show every extreme that they name: couplings[0] is zero.
All inputs are finite; a program needn't handle non-finite values. Where the computation divides by a largest or mean magnitude, that divisor is 1e-20 or more.
Results may differ from a plain program's by a relative error of at most 0.0001.
Values sent between devices are 32-bit elements; how exact they have to be, the bound alone decides.
No kernel may reach another device: no remote copies, remote signals or barrier semaphores. Data moves between devices by JAX's collectives and lax.ppermute only.
A program may use at most 64 MiB of HBM per device.

v0:
```python
import jax
import jax.numpy as jnp
from jax import lax
from jax.sharding import PartitionSpec as P

ITERS = 12
LEVELS = 2


def passed_along(block, axis, distance):
    devices = range(lax.axis_size(axis))
    route = [(i - distance, i) for i in devices if i - distance in devices]
    return lax.ppermute(block, axis, route)


def product(left, right):
    return jnp.matmul(left, right, precision=lax.Precision.HIGHEST)


def flipped(matrix):
    return jnp.swapaxes(matrix, -1, -2)


def spread_columns(columns):
    return lax.all_gather(columns, "rhs", axis=2, tiled=True)


def column_inverse(blocks):
    order = blocks.shape[-1]
    width = order // lax.axis_size("rhs")
    identity = jnp.eye(order, dtype=jnp.float32)
    row_bound = jnp.max(jnp.sum(jnp.abs(blocks), axis=-1), axis=-1)
    start_cols = lax.dynamic_slice_in_dim(identity, lax.axis_index("rhs") * width, width, 1)
    start_guess = start_cols[None] / row_bound[:, None, None]

    def sweep(counter, columns):
        whole = spread_columns(columns)
        return 2.0 * columns - product(whole, product(blocks, columns))

    columns = lax.fori_loop(0, ITERS, sweep, start_guess)
    return spread_columns(columns)


def next_terms(link, inverse, multiplier, weighted, solved):
    return (
        product(product(link, inverse), link.T),
        -product(link, multiplier),
        product(weighted, link.T),
        product(link, solved),
    )


def per_device(diag_blocks, couplings, arrow_coupling, right_sides, arrow_block, arrow_rhs):
    count = diag_blocks.shape[0]
    diagonal = [diag_blocks[j] for j in range(count)]
    coupling = [couplings[j] for j in range(count)]
    arrow = [arrow_coupling[j] for j in range(count)]
    right = [right_sides[j] for j in range(count)]
    results = [[None] * count for whole in range(4)]
    block_total = jnp.zeros(arrow_block.shape, jnp.float32)
    right_total = jnp.zeros(arrow_rhs.shape, jnp.float32)
    for level_no in range(LEVELS):
        stride = 2**level_no
        gone_list = list(range(stride, count, 2 * stride))
        kept_list = list(range(0, count, 2 * stride))
        stacked = jnp.stack([diagonal[j] for j in gone_list])
        own_link = jnp.stack([coupling[j] for j in gone_list])
        own_arrow = jnp.stack([arrow[j] for j in gone_list])
        own_right = jnp.stack([right[j] for j in gone_list])
        inverse = column_inverse(stacked)
        multiplier = product(inverse, own_link)
        solved = product(inverse, own_right)
        weighted = product(own_arrow, inverse)
        left_diag = product(flipped(own_link), multiplier)
        left_right = product(flipped(own_link), solved)
        left_arrow = product(weighted, own_link)
        full_arrow, full_weighted = (
            lax.all_gather(own_arrow, "rhs", axis=1, tiled=True),
            lax.all_gather(weighted, "rhs", axis=1, tiled=True),
        )
        block_part = jnp.sum(product(weighted, flipped(full_arrow)), axis=0)
        right_part = jnp.sum(product(full_weighted, own_right), axis=0)
        block_sum, right_sum = lax.psum((block_part, right_part), "tm")
        block_total = block_total + block_sum
        right_total = right_total + right_sum
        last = len(gone_list) - 1
        far_link = passed_along(coupling[0], "tm", -1)
        far_terms = next_terms(
            far_link, inverse[last], multiplier[last], weighted[last], solved[last]
        )
        from_before = passed_along(
            (far_terms[0], far_terms[1], far_terms[2], far_terms[3]), "tm", 1
        )
        new_diag = list(diagonal)
        new_link = list(coupling)
        new_arrow = list(arrow)
        new_right = list(right)
        for place, kept in enumerate(kept_list):
            if kept == 0:
                before = from_before
            else:
                idx = place - 1
                before = next_terms(
                    coupling[kept], inverse[idx], multiplier[idx], weighted[idx], solved[idx]
                )
            new_diag[kept] = diagonal[kept] - before[0] - left_diag[place]
            new_link[kept] = before[1]
            new_arrow[kept] = arrow[kept] - before[2] - left_arrow[place]
            new_right[kept] = right[kept] - before[3] - left_right[place]
        for idx, gone in enumerate(gone_list):
            results[0][gone] = inverse[idx]
            results[1][gone] = multiplier[idx]
            results[2][gone] = weighted[idx]
            results[3][gone] = solved[idx]
        diagonal, coupling, arrow, right = (new_diag, new_link, new_arrow, new_right)
    kept = 0
    results[0][kept] = diagonal[kept]
    results[1][kept] = coupling[kept]
    results[2][kept] = arrow[kept]
    results[3][kept] = right[kept]
    return (
        jnp.stack(results[0]),
        jnp.stack(results[1]),
        jnp.stack(results[2]),
        jnp.stack(results[3]),
        arrow_block - block_total,
        arrow_rhs - right_total,
    )


def solution(mesh):
    return jax.shard_map(
        per_device,
        mesh=mesh,
        in_specs=(
            P("tm", None, None),
            P("tm", None, None),
            P("tm", "rhs", None),
            P("tm", None, "rhs"),
            P("rhs", None),
            P(None, "rhs"),
        ),
        out_specs=(
            P("tm", None, None),
            P("tm", None, None),
            P("tm", "rhs", None),
            P("tm", None, "rhs"),
            P("rhs", None),
            P(None, "rhs"),
        ),
        check_vma=False,
    )
```

profile of v0, /device:TPU:8, one launch (start us, length us, event | category | flops | bytes accessed | tf_op | source)
XLA Modules:
  0.0 714.3 jit_solution(15085392077638419299)
XLA Ops:
  10.0 262.6 %while.20 = (s32[]{:T(128)}, f32[2,384,192]{1,2,0:T(8,128)S(1)}, f32[2,384,384]{2,1,0:T(8,128)S(1)}, s32[]{:T(128)}) while((s32[]{:T(128)}, f32[2,384,192]{1,2,0:T(8,128)S(1)}, f32[2,384,384]{2,1,0:T(8,128)S(1)}, s32[]{:T(128)}) %tuple.50), condition=%wide.region_3.0_spmd, body=%wide.region_2.0_spmd.sunk | while | flops 1359249408 | bytes 15335573 | solution.py:40
  13.5 17.2 %all-gather.7.cloned.1.call-done = f32[2,384,384]{1,2,0:T(8,128)} async-done(((f32[2,384,192]{1,2,0:T(8,128)}), f32[2,384,384]{1,2,0:T(8,128)}) %all-gather.7.cloned.1.call-update) | async-done | bytes 1179664 | tf_op jit(solution)/shard_map/while/body/eval_jaxpr/all_gather | solution.py:25
  37.0 15.6 %all-gather.7.cloned.1.call-done = f32[2,384,384]{1,2,0:T(8,128)} async-done(((f32[2,384,192]{1,2,0:T(8,128)}), f32[2,384,384]{1,2,0:T(8,128)}) %all-gather.7.cloned.1.call-update) | async-done | bytes 1179664 | tf_op jit(solution)/shard_map/while/body/eval_jaxpr/all_gather | solution.py:25
  58.9 15.6 %all-gather.7.cloned.1.call-done = f32[2,384,384]{1,2,0:T(8,128)} async-done(((f32[2,384,192]{1,2,0:T(8,128)}), f32[2,384,384]{1,2,0:T(8,128)}) %all-gather.7.cloned.1.call-update) | async-done | bytes 1179664 | tf_op jit(solution)/shard_map/while/body/eval_jaxpr/all_gather | solution.py:25
  80.8 15.3 %all-gather.7.cloned.1.call-done = f32[2,384,384]{1,2,0:T(8,128)} async-done(((f32[2,384,192]{1,2,0:T(8,128)}), f32[2,384,384]{1,2,0:T(8,128)}) %all-gather.7.cloned.1.call-update) | async-done | bytes 1179664 | tf_op jit(solution)/shard_map/while/body/eval_jaxpr/all_gather | solution.py:25
  102.3 15.3 %all-gather.7.cloned.1.call-done = f32[2,384,384]{1,2,0:T(8,128)} async-done(((f32[2,384,192]{1,2,0:T(8,128)}), f32[2,384,384]{1,2,0:T(8,128)}) %all-gather.7.cloned.1.call-update) | async-done | bytes 1179664 | tf_op jit(solution)/shard_map/while/body/eval_jaxpr/all_gather | solution.py:25
  123.9 15.3 %all-gather.7.cloned.1.call-done = f32[2,384,384]{1,2,0:T(8,128)} async-done(((f32[2,384,192]{1,2,0:T(8,128)}), f32[2,384,384]{1,2,0:T(8,128)}) %all-gather.7.cloned.1.call-update) | async-done | bytes 1179664 | tf_op jit(solution)/shard_map/while/body/eval_jaxpr/all_gather | solution.py:25
  145.5 15.6 %all-gather.7.cloned.1.call-done = f32[2,384,384]{1,2,0:T(8,128)} async-done(((f32[2,384,192]{1,2,0:T(8,128)}), f32[2,384,384]{1,2,0:T(8,128)}) %all-gather.7.cloned.1.call-update) | async-done | bytes 1179664 | tf_op jit(solution)/shard_map/while/body/eval_jaxpr/all_gather | solution.py:25
  167.4 15.6 %all-gather.7.cloned.1.call-done = f32[2,384,384]{1,2,0:T(8,128)} async-done(((f32[2,384,192]{1,2,0:T(8,128)}), f32[2,384,384]{1,2,0:T(8,128)}) %all-gather.7.cloned.1.call-update) | async-done | bytes 1179664 | tf_op jit(solution)/shard_map/while/body/eval_jaxpr/all_gather | solution.py:25
  189.3 15.6 %all-gather.7.cloned.1.call-done = f32[2,384,384]{1,2,0:T(8,128)} async-done(((f32[2,384,192]{1,2,0:T(8,128)}), f32[2,384,384]{1,2,0:T(8,128)}) %all-gather.7.cloned.1.call-update) | async-done | bytes 1179664 | tf_op jit(solution)/shard_map/while/body/eval_jaxpr/all_gather | solution.py:25
  211.1 15.3 %all-gather.7.cloned.1.call-done = f32[2,384,384]{1,2,0:T(8,128)} async-done(((f32[2,384,192]{1,2,0:T(8,128)}), f32[2,384,384]{1,2,0:T(8,128)}) %all-gather.7.cloned.1.call-update) | async-done | bytes 1179664 | tf_op jit(solution)/shard_map/while/body/eval_jaxpr/all_gather | solution.py:25
  232.7 15.6 %all-gather.7.cloned.1.call-done = f32[2,384,384]{1,2,0:T(8,128)} async-done(((f32[2,384,192]{1,2,0:T(8,128)}), f32[2,384,384]{1,2,0:T(8,128)}) %all-gather.7.cloned.1.call-update) | async-done | bytes 1179664 | tf_op jit(solution)/shard_map/while/body/eval_jaxpr/all_gather | solution.py:25
  254.6 15.3 %all-gather.7.cloned.1.call-done = f32[2,384,384]{1,2,0:T(8,128)} async-done(((f32[2,384,192]{1,2,0:T(8,128)}), f32[2,384,384]{1,2,0:T(8,128)}) %all-gather.7.cloned.1.call-update) | async-done | bytes 1179664 | tf_op jit(solution)/shard_map/while/body/eval_jaxpr/all_gather | solution.py:25
  276.4 7.3 %collective-permute-start = (f32[384,384]{1,0:T(8,128)}, f32[384,384]{1,0:T(8,128)S(1)}, u32[]{:S(2)}, u32[]{:S(2)}) collective-permute-start(f32[384,384]{1,0:T(8,128)} %get-tuple-element.65), channel_id=1, source_target_pairs={{2,0},{4,2},{6,4},{8,6},{10,8},{12,10},{14,12},{16,14},{18,16},{20... | collective-permute-start | bytes 1769480 | tf_op jit(solution)/shard_map/ppermute | solution.py:13
  299.1 3.6 fusion.15
  317.1 4.1 fusion.30
  326.3 3.8 abs_reduce_fusion.1
  334.5 46.9 %while.21 = (s32[]{:T(128)}, f32[1,384,192]{1,2,0:T(8,128)S(1)}, f32[384,384]{1,0:T(8,128)S(1)}, s32[]{:T(128)}) while((s32[]{:T(128)}, f32[1,384,192]{1,2,0:T(8,128)S(1)}, f32[384,384]{1,0:T(8,128)S(1)}, s32[]{:T(128)}) %tuple.53), condition=%wide.region_7.0_spmd, body=%wide.region_6.0_spmd.sunk | while | flops 679624704 | bytes 3538997 | solution.py:40
  408.5 3.6 collective-permute-start.1
  414.2 4.7 collective-permute-start.2
  425.8 16.9 %collective-permute-done.2 = f32[384,384]{0,1:T(8,128)} collective-permute-done((f32[384,384]{0,1:T(8,128)S(1)}, f32[384,384]{0,1:T(8,128)}, u32[]{:S(2)}, u32[]{:S(2)}) %collective-permute-start.2) | collective-permute-done | bytes 589856 | tf_op jit(solution)/shard_map/ppermute | solution.py:13
  447.6 210.5 %all-reduce.3.cloned.1.call-done = (f32[128,256]{1,0:T(8,128)}, f32[256,64]{0,1:T(8,128)}) async-done(((f32[128,256]{1,0:T(8,128)}, f32[256,64]{0,1:T(8,128)}), (f32[128,256]{1,0:T(8,128)}, f32[256,64]{0,1:T(8,128)})) %all-reduce.3.cloned.1.call-update) | async-done | bytes 196624 | tf_op jit(solution)/shard_map/psum | solution.py:83
  675.6 3.9 collective-permute-start.4
  683.4 18.5 %collective-permute-done.4 = f32[384,384]{1,0:T(8,128)S(1)} collective-permute-done((f32[384,384]{1,0:T(8,128)S(1)}, f32[384,384]{1,0:T(8,128)S(1)}, u32[]{:S(2)}, u32[]{:S(2)}) %collective-permute-start.4) | collective-permute-done | bytes 589856 | tf_op jit(solution)/shard_map/ppermute | solution.py:13
  (296 shorter events, 233.1 us)
Async XLA Ops:
  10.0 20.7 %all-gather.7.cloned.1.call-start = ((), (), s32[]{:S(2)}) async-start(), calls=%async_computation.2 | async-start | bytes 1769472 | tf_op jit(solution)/shard_map/while/body/eval_jaxpr/all_gather | solution.py:25
  33.5 19.1 %all-gather.7.cloned.1.call-start = ((), (), s32[]{:S(2)}) async-start(), calls=%async_computation.2 | async-start | bytes 1769472 | tf_op jit(solution)/shard_map/while/body/eval_jaxpr/all_gather | solution.py:25
  55.4 19.1 %all-gather.7.cloned.1.call-start = ((), (), s32[]{:S(2)}) async-start(), calls=%async_computation.2 | async-start | bytes 1769472 | tf_op jit(solution)/shard_map/while/body/eval_jaxpr/all_gather | solution.py:25
  77.3 18.8 %all-gather.7.cloned.1.call-start = ((), (), s32[]{:S(2)}) async-start(), calls=%async_computation.2 | async-start | bytes 1769472 | tf_op jit(solution)/shard_map/while/body/eval_jaxpr/all_gather | solution.py:25
  98.8 18.8 %all-gather.7.cloned.1.call-start = ((), (), s32[]{:S(2)}) async-start(), calls=%async_computation.2 | async-start | bytes 1769472 | tf_op jit(solution)/shard_map/while/body/eval_jaxpr/all_gather | solution.py:25
  120.4 18.8 %all-gather.7.cloned.1.call-start = ((), (), s32[]{:S(2)}) async-start(), calls=%async_computation.2 | async-start | bytes 1769472 | tf_op jit(solution)/shard_map/while/body/eval_jaxpr/all_gather | solution.py:25
  142.0 19.1 %all-gather.7.cloned.1.call-start = ((), (), s32[]{:S(2)}) async-start(), calls=%async_computation.2 | async-start | bytes 1769472 | tf_op jit(solution)/shard_map/while/body/eval_jaxpr/all_gather | solution.py:25
  163.9 19.1 %all-gather.7.cloned.1.call-start = ((), (), s32[]{:S(2)}) async-start(), calls=%async_computation.2 | async-start | bytes 1769472 | tf_op jit(solution)/shard_map/while/body/eval_jaxpr/all_gather | solution.py:25
  185.7 19.1 %all-gather.7.cloned.1.call-start = ((), (), s32[]{:S(2)}) async-start(), calls=%async_computation.2 | async-start | bytes 1769472 | tf_op jit(solution)/shard_map/while/body/eval_jaxpr/all_gather | solution.py:25
  207.6 18.8 %all-gather.7.cloned.1.call-start = ((), (), s32[]{:S(2)}) async-start(), calls=%async_computation.2 | async-start | bytes 1769472 | tf_op jit(solution)/shard_map/while/body/eval_jaxpr/all_gather | solution.py:25
  229.2 19.1 %all-gather.7.cloned.1.call-start = ((), (), s32[]{:S(2)}) async-start(), calls=%async_computation.2 | async-start | bytes 1769472 | tf_op jit(solution)/shard_map/while/body/eval_jaxpr/all_gather | solution.py:25
  251.1 18.8 %all-gather.7.cloned.1.call-start = ((), (), s32[]{:S(2)}) async-start(), calls=%async_computation.2 | async-start | bytes 1769472 | tf_op jit(solution)/shard_map/while/body/eval_jaxpr/all_gather | solution.py:25
  272.6 18.6 %all-gather.5.cloned.1.call-start = ((), (), s32[]{:S(2)}) async-start(), calls=%async_computation | async-start | bytes 1769472 | tf_op jit(solution)/shard_map/all_gather | solution.py:25
  274.0 384.1 %all-reduce.3.cloned.1.call-start = ((), (), s32[]{:S(2)}) async-start(), calls=%async_computation.1 | async-start | bytes 393216 | tf_op jit(solution)/shard_map/psum | solution.py:83
  276.4 117.4 %collective-permute-start = (f32[384,384]{1,0:T(8,128)}, f32[384,384]{1,0:T(8,128)S(1)}, u32[]{:S(2)}, u32[]{:S(2)}) collective-permute-start(f32[384,384]{1,0:T(8,128)} %get-tuple-element.65), channel_id=1, source_target_pairs={{2,0},{4,2},{6,4},{8,6},{10,8},{12,10},{14,12},{16,14},{18,16},{20... | collective-permute-start | bytes 1769480 | tf_op jit(solution)/shard_map/ppermute | solution.py:13
  395.2 277.8 %collective-permute-start.8 = (f32[384,64]{0,1:T(8,128)}, f32[384,64]{0,1:T(8,128)}, u32[]{:S(2)}, u32[]{:S(2)}) collective-permute-start(f32[384,64]{0,1:T(8,128)} %convolution_bitcast_fusion.4), channel_id=1, source_target_pairs={{0,2},{2,4},{4,6},{6,8},{8,10},{10,12},{12,14},{14,16},{16,18},{18... | collective-permute-start | bytes 294920 | tf_op jit(solution)/shard_map/ppermute | solution.py:13
  400.1 281.2 %collective-permute-start.6 = (f32[128,384]{1,0:T(8,128)}, f32[128,384]{1,0:T(8,128)}, u32[]{:S(2)}, u32[]{:S(2)}) collective-permute-start(f32[128,384]{1,0:T(8,128)} %fusion.58), channel_id=1, source_target_pairs={{0,2},{2,4},{4,6},{6,8},{8,10},{10,12},{12,14},{14,16},{16,18},{18... | collective-permute-start | bytes 589832 | tf_op jit(solution)/shard_map/ppermute | solution.py:13
  408.5 274.9 %collective-permute-start.1 = (f32[384,384]{1,0:T(8,128)}, f32[384,384]{1,0:T(8,128)}, u32[]{:S(2)}, u32[]{:S(2)}) collective-permute-start(f32[384,384]{1,0:T(8,128)} %fusion.86), channel_id=1, source_target_pairs={{0,2},{2,4},{4,6},{6,8},{8,10},{10,12},{12,14},{14,16},{16,18},{18... | collective-permute-start | bytes 1769480 | tf_op jit(solution)/shard_map/ppermute | solution.py:13
  414.2 28.5 %collective-permute-start.2 = (f32[384,384]{0,1:T(8,128)S(1)}, f32[384,384]{0,1:T(8,128)}, u32[]{:S(2)}, u32[]{:S(2)}) collective-permute-start(f32[384,384]{0,1:T(8,128)S(1)} %fusion.6), channel_id=1, source_target_pairs={{0,2},{2,4},{4,6},{6,8},{8,10},{10,12},{12,14},{14,16},{16,18},{18... | collective-permute-start | bytes 1769480 | tf_op jit(solution)/shard_map/ppermute | solution.py:13
  442.7 218.5 %collective-permute-start.3 = (f32[384,384]{0,1:T(8,128)}, f32[384,384]{0,1:T(8,128)S(1)}, u32[]{:S(2)}, u32[]{:S(2)}) collective-permute-start(f32[384,384]{0,1:T(8,128)} %collective-permute-done.2), channel_id=1, source_target_pairs={{2,0},{4,2},{6,4},{8,6},{10,8},{12,10},{14,12},{16,14},{18,16},{20... | collective-permute-start | bytes 1769480 | tf_op jit(solution)/shard_map/ppermute | solution.py:13
  661.7 13.9 %collective-permute-start.9 = (f32[384,64]{0,1:T(8,128)S(1)}, f32[384,64]{0,1:T(8,128)S(1)}, u32[]{:S(2)}, u32[]{:S(2)}) collective-permute-start(f32[384,64]{0,1:T(8,128)S(1)} %fusion.91), channel_id=1, source_target_pairs={{0,2},{2,4},{4,6},{6,8},{8,10},{10,12},{12,14},{14,16},{16,18},{18... | collective-permute-start | bytes 294920 | tf_op jit(solution)/shard_map/ppermute | solution.py:13
  664.9 16.4 %collective-permute-start.7 = (f32[128,384]{1,0:T(8,128)S(1)}, f32[128,384]{1,0:T(8,128)S(1)}, u32[]{:S(2)}, u32[]{:S(2)}) collective-permute-start(f32[128,384]{1,0:T(8,128)S(1)} %fusion.89), channel_id=1, source_target_pairs={{0,2},{2,4},{4,6},{6,8},{8,10},{10,12},{12,14},{14,16},{16,18},{18... | collective-permute-start | bytes 589832 | tf_op jit(solution)/shard_map/ppermute | solution.py:13
  673.0 32.1 %collective-permute-start.5 = (f32[384,384]{1,0:T(8,128)S(1)}, f32[384,384]{1,0:T(8,128)S(1)}, u32[]{:S(2)}, u32[]{:S(2)}) collective-permute-start(f32[384,384]{1,0:T(8,128)S(1)} %convolution_negate_fusion), channel_id=1, source_target_pairs={{0,2},{2,4},{4,6},{6,8},{8,10},{10,12},{12,14},{14,16},{16,18},{18... | collective-permute-start | bytes 1769480 | tf_op jit(solution)/shard_map/ppermute | solution.py:13
  675.6 26.4 %collective-permute-start.4 = (f32[384,384]{1,0:T(8,128)S(1)}, f32[384,384]{1,0:T(8,128)S(1)}, u32[]{:S(2)}, u32[]{:S(2)}) collective-permute-start(f32[384,384]{1,0:T(8,128)S(1)} %fusion.87), channel_id=1, source_target_pairs={{0,2},{2,4},{4,6},{6,8},{8,10},{10,12},{12,14},{14,16},{16,18},{18... | collective-permute-start | bytes 1769480 | tf_op jit(solution)/shard_map/ppermute | solution.py:13
  (64 other events, 1212.6 us)
Sparse Core Ops, SparseCore 0:
  13.2 17.4 all-gather.6
  36.7 15.8 all-gather.6
  58.6 15.8 all-gather.6
  80.1 15.8 all-gather.6
  101.7 15.8 all-gather.6
  123.3 15.8 all-gather.6
  145.2 15.8 all-gather.6
  167.1 15.8 all-gather.6
  188.9 15.8 all-gather.6
  210.5 15.8 all-gather.6
  232.4 15.8 all-gather.6
  253.9 15.8 all-gather.6
Sparse Core Ops, SparseCore 1:
  275.5 15.7 all-gather.4
  446.3 211.7 all-reduce.2
where the time goes:
time: 721 us; the launch traced here: 714 us
  waiting for transfers between devices  435 us (60%)
  matrix products  139 us (19%)
  blocking collectives  39 us (5%)
  starting transfers between devices  37.8 us (5%)
  local copies, waits for them, and re-layouts  32.2 us (4%)
  between operations  16.4 us (2%)
  other arithmetic  13.3 us (2%)
    psum x1, waiting for transfers between devices, per_device(): block_sum, right_sum = lax.psum((block_part, right_part), 'tm')  211 us
    all_gather x13, waiting for transfers between devices, spread_columns(): return lax.all_gather(columns, 'rhs', axis=2, tiled=True)  189 us
    dot_general x79, matrix products, product(): return jnp.matmul(left, right, precision=lax.Precision.HIGHEST)  139 us
    ppermute x10, starting transfers between devices, passed_along(): return lax.ppermute(block, axis, route)  37.2 us
    ppermute x10, waiting for transfers between devices, passed_along(): return lax.ppermute(block, axis, route)  35.5 us
    all_gather x13, blocking collectives, spread_columns(): return lax.all_gather(columns, 'rhs', axis=2, tiled=True)  29 us
  transfers between devices with their start and end apart: 24, of which 16 were waited for; matrix products, arithmetic and copies ran while one was open for 19% of the time, Pallas kernels for 0%

commit v1 on v0

v1 whole, which is shorter than its diff:
```python
import jax
import jax.numpy as jnp
from jax import lax
from jax.experimental import pallas as pl
from jax.experimental.pallas import tpu as pltpu
from jax.sharding import PartitionSpec as P


ITERS = 12
N = 384
HALF = 192
ROWS = 128
COLS = 64
F32 = jnp.float32
B16 = jnp.bfloat16
VMEM = 67043328
ROOM = 600 << 10


def dot(a, b, nt):
    dims = (((1,), (1 if nt else 0,)), ((), ()))
    return lax.dot_general(a, b, dims, preferred_element_type=F32)


def parts(x):
    high = x.astype(B16)
    return high, (x - high.astype(F32)).astype(B16)


def mm(a, b, nt=False):
    ah, al = parts(a)
    bh, bl = parts(b)
    n = b.shape[0] if nt else b.shape[1]
    if n % 128 == 0:
        both = dot(ah, jnp.concatenate([bh, bl], 0 if nt else 1), nt)
        return both[:, :n] + (both[:, n:] + dot(al, bh, nt))
    return dot(ah, bh, nt) + (dot(ah, bl, nt) + dot(al, bh, nt))


def newton(m_ref, x_ref):
    m = m_ref[...]
    row_bound = jnp.max(jnp.sum(jnp.abs(m), axis=1, keepdims=True), axis=0, keepdims=True)
    scale = 1.0 / row_bound
    eye = (
        lax.broadcasted_iota(jnp.int32, (N, N), 0) == lax.broadcasted_iota(jnp.int32, (N, N), 1)
    ).astype(F32)
    x_ref[...] = 2.0 * (eye * scale) - (m * scale) * scale

    def sweep(counter, carry):
        x = x_ref[...]
        residual = eye - mm(m_ref[...], x)
        x_ref[...] = x + mm(x, residual)
        return carry

    lax.fori_loop(0, ITERS - 1, sweep, 0)


class Feed:
    def __init__(self, core, sources, buf, sem):
        self.copy = pltpu.make_async_copy(sources[0], buf, sem)
        self.buf = buf
        self.ready = False
        if len(sources) == 1:
            self.copy.start()
        else:
            for which, source in enumerate(sources):

                @pl.when(core == which)
                def _(source=source):
                    pltpu.make_async_copy(source, buf, sem).start()

    def ref(self):
        if not self.ready:
            self.copy.wait()
            self.ready = True
        return self.buf

    def get(self):
        return self.ref()[...]


class Drain:
    def __init__(self, sems):
        self.sems = sems
        self.copies = []

    def send(self, src, dst):
        copy = pltpu.make_async_copy(src, dst, self.sems.at[len(self.copies)])
        copy.start()
        self.copies.append(copy)

    def finish(self):
        for copy in self.copies:
            copy.wait()


OUT_COPIES = 16


def call(body, me, ins, outs, scratch=(), units=1.0, alias=None, room=0):
    arrays = []
    places = []
    for shape, sources in ins:
        found = []
        for array, view in sources:
            for number, known in enumerate(arrays):
                if known is array:
                    break
            else:
                number = len(arrays)
                arrays.append(array)
            found.append((number, view))
        places.append(found)
    count = len(arrays)
    extra = list(alias or ())

    def kernel(core_ref, *refs):
        core = core_ref[0]
        given = refs[:count]
        outputs = refs[count + len(extra) : count + len(extra) + len(outs)]
        rest = refs[count + len(extra) + len(outs) :]
        bufs, held, in_sems, out_sems = rest[: len(ins)], rest[len(ins) : -2], rest[-2], rest[-1]
        feeds = [
            Feed(core, [view(given[number], core) for number, view in found], buf, in_sems.at[i])
            for i, (found, buf) in enumerate(zip(places, bufs))
        ]
        drain = Drain(out_sems)
        body(core, feeds, outputs, held, drain)
        drain.finish()

    moved = sum(4 * a.size for a in arrays)
    far = pl.BlockSpec(memory_space=pltpu.HBM)
    return pl.pallas_call(
        kernel,
        out_shape=[jax.ShapeDtypeStruct(shape, F32) for shape in outs],
        in_specs=[pl.BlockSpec(memory_space=pltpu.SMEM)] + [far] * (count + len(extra)),
        out_specs=[far] * len(outs),
        scratch_shapes=[pltpu.VMEM(shape, F32) for shape, sources in ins]
        + [pltpu.VMEM(shape, F32) for shape in scratch]
        + [pltpu.SemaphoreType.DMA((len(ins),)), pltpu.SemaphoreType.DMA((OUT_COPIES,))],
        input_output_aliases={1 + count + i: i for i in range(len(extra))},
        compiler_params=pltpu.CompilerParams(vmem_limit_bytes=VMEM - room),
        cost_estimate=pl.CostEstimate(flops=int(units * 6 * N**3), bytes_accessed=moved, transcendentals=0),
    )(me, *arrays, *extra)


def whole(ref, core):
    return ref


def rows(start, size):
    return lambda ref, core: ref.at[pl.ds(start, size)]


def at(index):
    return lambda ref, core: ref.at[index]


def own(ref, core):
    return ref.at[1 + 2 * core]


def core_rows(core, size):
    mine = pl.multiple_of(core * size, size)
    other = pl.multiple_of((1 - core) * size, size)
    return pl.ds(mine, size), pl.ds(other, size)


def inverse_body(core, ins, outs, held, drain):
    d, l, l0 = ins
    x_out, t_out, w_out, l0_out = outs
    x_s, t_s, w_s = held
    drain.send(l0.ref(), l0_out)
    newton(d.ref(), x_s)
    drain.send(x_s, x_out)
    l_ref = l.ref()

    @pl.when(core == 0)
    def _():
        w_s[...] = l_ref[...]

    @pl.when(core == 1)
    def _():
        w_s[...] = l_ref[...].T

    drain.send(w_s, w_out)
    w = w_s[...]
    t_s[...] = mm(mm(w, x_s[...]), w, nt=True)
    drain.send(t_s, t_out)


def own_body(core, ins, outs, held, drain):
    x_in, c_in, cx_in, b_in, bx_in, l_in, w_in = ins
    snd, keep = outs
    full, b_s, vz_s, gh_s, blk_s, y_s = held
    mine, other = core_rows(core, ROWS)
    full[mine, :] = c_in.get()
    full[other, :] = cx_in.get()
    b_s[0:COLS, :] = b_in.get()
    b_s[COLS:, :] = bx_in.get()
    x = x_in.get()
    drain.send(x_in.ref(), snd.at[pl.ds(0, N)])
    c = full[...]
    vz_s[0:256, :] = mm(c, x)
    vz_s[256:384, :] = mm(b_s[...], x, nt=True)
    drain.send(vz_s.at[other], snd.at[pl.ds(1024, ROWS)])
    drain.send(vz_s.at[pl.ds(320, COLS)], snd.at[pl.ds(1152, COLS)])
    drain.send(vz_s.at[mine], keep.at[pl.ds(0, ROWS)])
    drain.send(vz_s.at[pl.ds(256, COLS)], keep.at[pl.ds(128, COLS)])
    y_s[...] = mm(x, l_in.get())
    drain.send(y_s, snd.at[pl.ds(N, N)])
    vz = vz_s[...]
    gh_s[...] = mm(vz, w_in.get(), nt=True)
    drain.send(gh_s.at[pl.ds(0, 256)], snd.at[pl.ds(768, 256)])
    drain.send(gh_s.at[pl.ds(320, COLS)], snd.at[pl.ds(1216, COLS)])
    drain.send(gh_s.at[pl.ds(256, COLS)], keep.at[pl.ds(192, COLS)])
    blk_s[:, 0:256] = mm(vz, c, nt=True)
    drain.send(blk_s.at[other], snd.at[pl.ds(1280, ROWS)])
    drain.send(blk_s.at[pl.ds(320, COLS)], snd.at[pl.ds(1408, COLS)])
    drain.send(blk_s.at[mine], keep.at[pl.ds(256, ROWS)])
    drain.send(blk_s.at[pl.ds(256, COLS)], keep.at[pl.ds(384, COLS)])


def inverse2_body(core, ins, outs, held, drain):
    d, t, tx = ins
    m_s, x_s = held
    m_s[...] = d.get() - (t.get() + tx.get())
    newton(m_s, x_s)
    drain.send(x_s, outs[0])


def arrow_body(core, ins, outs, held, drain):
    x_in, c_in, cx_in, g, gx, b_in, hk, hr, bk, br, rk, rr = ins
    full, vz_s, s_s = held
    mine, other = core_rows(core, ROWS)
    full[mine, :] = c_in.get()
    full[other, :] = cx_in.get()
    full[...] = full[...] - (g.get() + gx.get())
    b = b_in.get() - (hk.get() + hr.get())
    x = x_in.get()
    vz_s[0:ROWS, :] = mm(full[mine, :], x)
    vz_s[ROWS:, :] = mm(b, x, nt=True)
    drain.send(vz_s, outs[0])
    sums = mm(vz_s[...], full[...], nt=True)
    s_s[0:ROWS, :] = sums[0:ROWS] + (bk.ref()[:, 0:256] + br.ref()[:, 0:256])
    s_s[ROWS:, :] = sums[ROWS:] + (rk.ref()[:, 0:256] + rr.ref()[:, 0:256])
    drain.send(s_s, outs[1])


def link_body(core, ins, outs, held, drain):
    l, y1, x2 = ins
    lp_s, y2_s = held
    lp_s[...] = -mm(l.get(), y1.get())
    drain.send(lp_s, outs[0])
    y2_s[...] = mm(x2.get(), lp_s[...])
    drain.send(y2_s, outs[1])


def next_body(core, ins, outs, held, drain):
    ln, y3, y2, x3, v3, z3, x2, vz2 = ins
    lnp_s, lnn_s, a_s, o_s = held
    out = outs[0]
    mine, _ = core_rows(core, HALF)
    lnp_s[...] = -mm(ln.get(), y3.get())
    lnn_s[...] = -mm(lnp_s[mine, :], y2.get())
    drain.send(lnn_s, out.at[pl.ds(HALF, HALF)])
    a_s[0:HALF, :] = mm(ln.ref()[mine, :], x3.get())
    a_s[HALF : HALF + ROWS, :] = v3.get()
    a_s[HALF + ROWS :, :] = z3.get()
    o_s[...] = mm(a_s[...], ln.get(), nt=True)
    a_s[0:HALF, :] = mm(lnp_s[mine, :], x2.get())
    a_s[HALF:, :] = vz2.get()
    o_s[...] = o_s[...] + mm(a_s[...], lnp_s[...], nt=True)
    drain.send(o_s.at[pl.ds(0, HALF)], out.at[pl.ds(0, HALF)])
    drain.send(o_s.at[pl.ds(HALF, HALF)], out.at[pl.ds(N, HALF)])


def left_body(core, ins, outs, held, drain):
    l1, y1, v1, z1, lp, y2, vz2, d, c, b = ins
    t_s, a_s, e_s = held
    mine, _ = core_rows(core, HALF)
    t_s[...] = l1.get().T
    e_s[0:HALF, :] = mm(t_s[mine, :], y1.get())
    a_s[0:ROWS, :] = v1.get()
    a_s[ROWS:, :] = z1.get()
    e_s[HALF:, :] = mm(a_s[...], l1.get())
    t_s[...] = lp.get().T
    e_s[0:HALF, :] = d.ref()[mine, :] - (e_s[0:HALF, :] + mm(t_s[mine, :], y2.get()))
    both = e_s[HALF:, :] + mm(vz2.get(), lp.get())
    e_s[HALF : HALF + ROWS, :] = c.get() - both[0:ROWS]
    e_s[HALF + ROWS :, :] = b.get() - both[ROWS:]
    drain.send(e_s, outs[0])


def place_body(core, ins, outs, held, drain):
    for feed, (out, which) in zip(ins, ((0, 1), (0, 3), (0, 2), (1, 1), (1, 3), (1, 2), (2, 1), (2, 3), (3, 1), (3, 3))):
        drain.send(feed.ref(), outs[out].at[which])
    vz2 = ins[10].ref()
    drain.send(vz2.at[pl.ds(0, ROWS)], outs[2].at[2])
    drain.send(vz2.at[pl.ds(ROWS, COLS)], outs[3].at[2])


def half_body(core, ins, outs, held, drain):
    e, n = ins
    h_s, r_s = held
    h_s[0:HALF, :] = e.ref()[0:HALF, :] - n.ref()[0:HALF, :]
    h_s[HALF:, :] = n.ref()[HALF : 2 * HALF, :]
    drain.send(h_s, outs[0])
    r_s[...] = e.ref()[HALF:, :] - n.ref()[N:, :]
    drain.send(r_s, outs[1])


def final_body(core, ins, outs, held, drain):
    top, right, s6, q6, q7, s8, q8 = ins
    sum_s, block_s, right_s = held
    a = s6.get() + q8.get()
    sum_s[...] = jnp.where(core == 0, s8.get() + q8.get(), a + (q6.get() + q7.get()))
    block_s[...] = top.get() - sum_s[0:ROWS]
    drain.send(block_s, outs[0])
    right_s[...] = right.get() - sum_s[ROWS:]
    drain.send(right_s, outs[1])


def kept_body(core, ins, outs, held, drain):
    h, hx, rest = ins
    mine, other = core_rows(core, HALF)
    for half, where in ((h, mine), (hx, other)):
        ref = half.ref()
        drain.send(ref.at[pl.ds(0, HALF)], outs[0].at[0, where])
        drain.send(ref.at[pl.ds(HALF, HALF)], outs[1].at[0, where])
    ref = rest.ref()
    drain.send(ref.at[pl.ds(0, ROWS)], outs[2].at[0])
    drain.send(ref.at[pl.ds(ROWS, COLS)], outs[3].at[0])


RINGS = {"y": (4, 32), "x": (4, 8), "z": (8, 1)}
ORDERS = (
    (("z", 0), ("z", 1), ("z", 0), ("z", 1), ("x", 0), ("x", 1), ("y", 0), ("y", 1)),
    (("x", 0), ("x", 1), ("y", 0), ("y", 1), ("z", 0), ("z", 1), ("z", 0), ("z", 1)),
)


def partner(index, ring, odd):
    size, stride = RINGS[ring]
    place = index // stride % size
    to = (place + (1 if place % 2 == odd else size - 1)) % size
    return index + (to - place) * stride


def step(value, number):
    route = []
    for index in range(lax.axis_size("tm")):
        for core in range(2):
            ring, odd = ORDERS[core][number]
            route.append((index * 2 + core, partner(index, ring, odd) * 2 + core))
    return lax.ppermute(value, ("tm", "rhs"), route)


def sum_over_tm(v, first):
    q1 = step(v, 0)
    a = v + q1
    q2 = step(a, 1)
    s3 = jnp.where(first, q2, a + q2)
    q3 = step(s3, 2)
    s4 = jnp.where(first, q3, s3 + q3)
    q4 = step(s4, 3)
    s5 = jnp.where(first, (a + q4) + (q2 + q3), s4 + q4)
    q5 = step(s5, 4)
    s6 = s5 + q5
    q6 = step(s6, 5)
    s7 = jnp.where(first, s6 + q6, q6)
    q7 = step(s7, 6)
    s8 = jnp.where(first, s7 + q7, q7)
    q8 = step(s8, 7)
    return s6, q6, q7, s8, q8


def swapped(value):
    return lax.ppermute(value, "rhs", [(0, 1), (1, 0)])


def along(value, distance, core=None):
    devices = range(lax.axis_size("tm"))
    pairs = [(i, i + distance) for i in devices if i + distance in devices]
    cores = (0, 1) if core is None else (core,)
    route = [(i * 2 + c, j * 2 + c) for i, j in pairs for c in cores]
    return lax.ppermute(value, ("tm", "rhs"), route)


def per_device(diag, link, arrow, right, arrow_block, arrow_rhs):
    core = lax.axis_index("rhs")
    first = core == 0
    me = jnp.reshape(core, (1,)).astype(jnp.int32)
    square = (N, N)
    right = jnp.swapaxes(right, 1, 2)
    arrow_x = swapped(arrow)
    right_x = swapped(right)

    strip = (ROWS, N)
    slim = (COLS, N)
    x, t, w, link_0 = call(
        inverse_body, me,
        [(square, [(diag, own)]), (square, [(link, lambda ref, c: ref.at[2 + c])]), (square, [(link, at(0))])],
        [square] * 4, scratch=[square] * 3, units=24,
    )
    t_x = swapped(t)
    link_n = along(link_0, -1)
    snd, keep = call(
        own_body, me,
        [
            (square, [(x, whole)]), (strip, [(arrow, own)]), (strip, [(arrow_x, own)]), (slim, [(right, own)]),
            (slim, [(right_x, own)]), (square, [(link, own)]), (square, [(w, whole)]),
        ],
        [(1472, N), (448, N)],
        scratch=[(256, N), (ROWS, N), square, square, square, square], units=4,
    )
    rcv = swapped(snd)
    (x2,) = call(
        inverse2_body, me,
        [(square, [(diag, at(2))]), (square, [(t, whole)]), (square, [(t_x, whole)])],
        [square], scratch=[square, square], units=22,
    )
    vz2, sums = call(
        arrow_body, me,
        [
            (square, [(x2, whole)]), (strip, [(arrow, at(2))]), (strip, [(arrow_x, at(2))]),
            ((256, N), [(snd, rows(768, 256))]), ((256, N), [(rcv, rows(768, 256))]), (slim, [(right, at(2))]),
            (slim, [(keep, rows(192, COLS))]), (slim, [(rcv, rows(1216, COLS))]),
            (strip, [(keep, rows(256, ROWS))]), (strip, [(rcv, rows(1280, ROWS))]),
            (slim, [(keep, rows(384, COLS))]), (slim, [(rcv, rows(1408, COLS))]),
        ],
        [(HALF, N), (HALF, 256)], scratch=[(256, N), (HALF, N), (HALF, 256)], units=2,
    )
    pieces = sum_over_tm(sums, first)

    x_1 = (square, [(snd, rows(0, N)), (rcv, rows(0, N))])
    x_3 = (square, [(rcv, rows(0, N)), (snd, rows(0, N))])
    y_1 = (square, [(snd, rows(N, N)), (rcv, rows(N, N))])
    y_3 = (square, [(rcv, rows(N, N)), (snd, rows(N, N))])
    v_1 = (strip, [(keep, rows(0, ROWS)), (rcv, rows(1024, ROWS))])
    v_3 = (strip, [(rcv, rows(1024, ROWS)), (keep, rows(0, ROWS))])
    z_1 = (slim, [(keep, rows(128, COLS)), (rcv, rows(1152, COLS))])
    z_3 = (slim, [(rcv, rows(1152, COLS)), (keep, rows(128, COLS))])
    x_2 = (square, [(x2, whole)])
    vz_2 = ((HALF, N), [(vz2, whole)])
    l_n = (square, [(link_n, whole)])
    link_p, y2 = call(
        link_body, me, [(square, [(link, at(2))]), y_1, x_2],
        [square, square], scratch=[square, square], room=ROOM, units=2,
    )
    l_p = (square, [(link_p, whole)])
    y_2 = (square, [(y2, whole)])
    (ahead,) = call(
        next_body, me, [l_n, y_3, y_2, x_3, v_3, z_3, x_2, vz_2],
        [(576, N)], scratch=[square, (HALF, N), square, square], room=ROOM, units=4.5,
    )
    behind1 = along(ahead, 1, 1)
    behind0 = along(ahead, 1, 0)
    (edge,) = call(
        left_body, me,
        [
            (square, [(link, at(1))]), y_1, v_1, z_1, l_p, y_2, vz_2,
            (square, [(diag, at(0))]), (strip, [(arrow, at(0))]), (slim, [(right, at(0))]),
        ],
        [square], scratch=[square, (HALF, N), square], room=ROOM, units=2,
    )
    placed = call(
        place_body, me, [x_1, x_3, x_2, y_1, y_3, y_2, v_1, v_3, z_1, z_3, vz_2],
        [(4, N, N), (4, N, N), (4, ROWS, N), (4, COLS, N)], room=ROOM, units=0.1,
    )
    halves, rest = call(
        half_body, me, [(square, [(edge, whole)]), ((576, N), [(behind0, whole), (behind1, whole)])],
        [square, (HALF, N)], scratch=[square, (HALF, N)], room=ROOM, units=0.1,
    )
    halves_x = swapped(halves)
    outs = call(
        kept_body, me,
        [(square, [(halves, whole)]), (square, [(halves_x, whole)]), ((HALF, N), [(rest, whole)])],
        [(4, N, N), (4, N, N), (4, ROWS, N), (4, COLS, N)], room=ROOM, units=0.1, alias=placed,
    )
    reduced, reduced_right = call(
        final_body, me,
        [((ROWS, 256), [(arrow_block, whole)]), ((COLS, 256), [(jnp.swapaxes(arrow_rhs, 0, 1), whole)])]
        + [((HALF, 256), [(piece, whole)]) for piece in pieces],
        [(ROWS, 256), (COLS, 256)], scratch=[(HALF, 256), (ROWS, 256), (COLS, 256)], room=ROOM, units=0.1,
    )
    return outs[0], outs[1], outs[2], jnp.swapaxes(outs[3], 1, 2), reduced, jnp.swapaxes(reduced_right, 0, 1)


def solution(mesh):
    placements = (P("tm", None, None), P("tm", None, None), P("tm", "rhs", None), P("tm", None, "rhs"),
                  P("rhs", None), P(None, "rhs"))
    return jax.shard_map(per_device, mesh=mesh, in_specs=placements, out_specs=placements, check_vma=False)
```

time: 721 us -> 143 us (0.20)
  the two profiles are of different devices: /device:TPU:8 before, /device:TPU:1 now
where the time goes in v1:
time: 143 us
  Pallas kernels  66.9 us (47%)
  starting transfers between devices  40.9 us (29%)
  waiting for transfers between devices  29.6 us (21%)
  other arithmetic  3.71 us (3%)
    pallas_call x11, Pallas kernels, call(): pl.pallas_call(kernel, out_shape=[jax.ShapeDtypeStruct(shape, F32) for sh...  66.9 us
    ppermute x8, waiting for transfers between devices, step(): return lax.ppermute(value, ('tm', 'rhs'), route)  24.5 us
    ppermute x8, starting transfers between devices, step(): return lax.ppermute(value, ('tm', 'rhs'), route)  19.5 us
    ppermute x5, starting transfers between devices, swapped(): return lax.ppermute(value, 'rhs', [(0, 1), (1, 0)])  16.3 us
    ppermute x3, starting transfers between devices, along(): return lax.ppermute(value, ('tm', 'rhs'), route)  5.1 us
    ppermute x5, waiting for transfers between devices, swapped(): return lax.ppermute(value, 'rhs', [(0, 1), (1, 0)])  5.08 us
  transfers between devices with their start and end apart: 16, of which 6 were waited for; matrix products, arithmetic and copies ran while one was open for 2% of the time, Pallas kernels for 39%

profile of v1, /device:TPU:1, one launch (start us, length us, event | category | flops | bytes accessed | tf_op | source)
XLA Modules:
  0.0 142.8 jit_solution(15623780109075202693)
XLA Ops:
  0.6 3.3 %collective-permute-start = (f32[4,128,384]{2,1,0:T(8,128)}, f32[4,128,384]{2,1,0:T(8,128)}, u32[]{:S(2)}, u32[]{:S(2)}) collective-permute-start(f32[4,128,384]{2,1,0:T(8,128)} %refs_8_.1), channel_id=1, source_target_pairs={{0,1},{1,0},{2,3},{3,2},{4,5},{5,4},{6,7},{7,6},{8,9},{9,8},{10,11... | collective-permute-start | bytes 2359304 | tf_op jit(solution)/shard_map/ppermute | solution.py:379
  4.0 17.6 %shard_map.109 = (f32[384,384]{1,0:T(8,128)}, f32[384,384]{1,0:T(8,128)}, f32[384,384]{1,0:T(8,128)}, f32[384,384]{1,0:T(8,128)}) custom-call(s32[1]{0:T(128)} %bitcast.core_ref, f32[4,384,384]{2,1,0:T(8,128)} %refs_7_.1, f32[4,384,384]{2,1,0:T(8,128)} %refs_0_.8), custom_call_target="tpu_custom_call" | custom-call | flops 8153726976 | bytes 4718592 | tf_op jit(solution)/shard_map/pallas_call | solution.py:133
  21.6 4.9 %shard_map.110 = (f32[1472,384]{1,0:T(8,128)}, f32[448,384]{1,0:T(8,128)}) custom-call(s32[1]{0:T(128)} %bitcast.core_ref, f32[384,384]{1,0:T(8,128)} %get-tuple-element.28.refs_0_, f32[4,128,384]{2,1,0:T(8,128)} %refs_8_.1, f32[4,128,384]{2,1,0:T(8,128)} %collective-permute-done.refs_2_, f32[4,64,384]{2,1,0:T(8,128)} %bitcast.6, ...), custom_call_target="tpu_custom_call" | custom-call | flops 1358954496 | bytes 5898240 | tf_op jit(solution)/shard_map/pallas_call | solution.py:133
  27.1 5.1 %collective-permute-done.3.refs_2_ = f32[384,384]{1,0:T(8,128)} collective-permute-done((f32[384,384]{1,0:T(8,128)}, f32[384,384]{1,0:T(8,128)}, u32[]{:S(2)}, u32[]{:S(2)}) %collective-permute-start.3) | collective-permute-done | bytes 589856 | tf_op jit(solution)/shard_map/ppermute | solution.py:379
  32.2 16.2 %shard_map.111.refs_3_.refs_0_.refs_5_.refs_2_ = f32[384,384]{1,0:T(8,128)} custom-call(s32[1]{0:T(128)} %bitcast.core_ref, f32[4,384,384]{2,1,0:T(8,128)} %refs_7_.1, f32[384,384]{1,0:T(8,128)} %get-tuple-element.32.refs_1_, f32[384,384]{1,0:T(8,128)} %collective-permute-done.3.refs_2_), custom_call_target="tpu_custom_call" | custom-call | flops 7474249728 | bytes 3538944 | tf_op jit(solution)/shard_map/pallas_call | solution.py:133
  48.4 3.5 %shard_map.113 = (f32[192,384]{1,0:T(8,128)}, f32[192,256]{1,0:T(8,128)}) custom-call(s32[1]{0:T(128)} %bitcast.core_ref, f32[384,384]{1,0:T(8,128)} %shard_map.111.refs_3_.refs_0_.refs_5_.refs_2_, f32[4,128,384]{2,1,0:T(8,128)} %refs_8_.1, f32[4,128,384]{2,1,0:T(8,128)} %collective-permute-done.refs_2_, ...), custom_call_target="tpu_custom_call" | custom-call | flops 679477248 | bytes 7766016 | tf_op jit(solution)/shard_map/pallas_call | solution.py:133
  52.0 5.0 %collective-permute-done.8 = f32[192,256]{1,0:T(8,128)S(1)} collective-permute-done((f32[192,256]{1,0:T(8,128)}, f32[192,256]{1,0:T(8,128)S(1)}, u32[]{:S(2)}, u32[]{:S(2)}) %collective-permute-start.8) | collective-permute-done | bytes 196640 | tf_op jit(solution)/shard_map/ppermute | solution.py:356
  60.1 3.7 %collective-permute-done.9 = f32[192,256]{1,0:T(8,128)S(1)} collective-permute-done((f32[192,256]{1,0:T(8,128)S(1)}, f32[192,256]{1,0:T(8,128)S(1)}, u32[]{:S(2)}, u32[]{:S(2)}) %collective-permute-start.9) | collective-permute-done | bytes 196640 | tf_op jit(solution)/shard_map/ppermute | solution.py:356
  63.8 3.7 %collective-permute-start.10 = (f32[192,256]{1,0:T(8,128)S(1)}, f32[192,256]{1,0:T(8,128)S(1)}, u32[]{:S(2)}, u32[]{:S(2)}) collective-permute-start(f32[192,256]{1,0:T(8,128)S(1)} %add_select_fusion.3), channel_id=1, source_target_pairs={{0,2},{1,65},{2,0},{3,67},{4,6},{5,69},{6,4},{7,71},{8,10},{9,73},... | collective-permute-start | bytes 589832 | tf_op jit(solution)/shard_map/ppermute | solution.py:356
  67.6 3.5 %collective-permute-done.10 = f32[192,256]{1,0:T(8,128)S(1)} collective-permute-done((f32[192,256]{1,0:T(8,128)S(1)}, f32[192,256]{1,0:T(8,128)S(1)}, u32[]{:S(2)}, u32[]{:S(2)}) %collective-permute-start.10) | collective-permute-done | bytes 196640 | tf_op jit(solution)/shard_map/ppermute | solution.py:356
  71.7 3.2 %collective-permute-start.11 = (f32[192,256]{1,0:T(8,128)}, f32[192,256]{1,0:T(8,128)}, u32[]{:S(2)}, u32[]{:S(2)}) collective-permute-start(f32[192,256]{1,0:T(8,128)} %add_select_fusion.2), channel_id=1, source_target_pairs={{0,14},{1,193},{2,4},{3,195},{4,2},{5,197},{6,8},{7,199},{8,6},{9,... | collective-permute-start | bytes 589832 | tf_op jit(solution)/shard_map/ppermute | solution.py:356
  74.9 3.6 %shard_map.112 = (f32[384,384]{1,0:T(8,128)}, f32[384,384]{1,0:T(8,128)}) custom-call(s32[1]{0:T(128)} %bitcast.core_ref, f32[4,384,384]{2,1,0:T(8,128)} %refs_0_.8, f32[1472,384]{1,0:T(8,128)} %get-tuple-element.30.refs_1_.refs_3_.refs_2_.refs_0_, f32[1472,384]{1,0:T(8,128)} %collective-permute-done.2.refs_2_.refs_4_.refs_1_, ...), custom_call_target="tpu_custom_call" | custom-call | flops 679477248 | bytes 7471104 | tf_op jit(solution)/shard_map/pallas_call | solution.py:133
  78.6 5.7 %shard_map.115 = f32[576,384]{1,0:T(8,128)} custom-call(s32[1]{0:T(128)} %bitcast.core_ref, f32[384,384]{1,0:T(8,128)} %collective-permute-done.4.refs_0_, f32[1472,384]{1,0:T(8,128)} %collective-permute-done.2.refs_2_.refs_4_.refs_1_, f32[1472,384]{1,0:T(8,128)} %get-tuple-element.30.refs_1_.refs_3_.refs_2_.refs_0_, ...), custom_call_target="tpu_custom_call" | custom-call | flops 1528823808 | bytes 7274496 | tf_op jit(solution)/shard_map/pallas_call | solution.py:133
  84.3 2.2 %collective-permute-start.6 = (f32[576,384]{1,0:T(8,128)}, f32[576,384]{1,0:T(8,128)}, u32[]{:S(2)}, u32[]{:S(2)}) collective-permute-start(f32[576,384]{1,0:T(8,128)} %shard_map.115), channel_id=1, source_target_pairs={{1,3},{3,5},{5,7},{7,9},{9,11},{11,13},{13,15},{15,17},{17,19},{19... | collective-permute-start | bytes 2654216 | tf_op jit(solution)/shard_map/ppermute | solution.py:387
  86.5 1.6 %collective-permute-start.5 = (f32[576,384]{1,0:T(8,128)}, f32[576,384]{1,0:T(8,128)}, u32[]{:S(2)}, u32[]{:S(2)}) collective-permute-start(f32[576,384]{1,0:T(8,128)} %shard_map.115), channel_id=1, source_target_pairs={{0,2},{2,4},{4,6},{6,8},{8,10},{10,12},{12,14},{14,16},{16,18},{18... | collective-permute-start | bytes 2654216 | tf_op jit(solution)/shard_map/ppermute | solution.py:387
  89.2 9.3 %collective-permute-done.12 = f32[192,256]{1,0:T(8,128)S(1)} collective-permute-done((f32[192,256]{1,0:T(8,128)S(1)}, f32[192,256]{1,0:T(8,128)S(1)}, u32[]{:S(2)}, u32[]{:S(2)}) %collective-permute-start.12) | collective-permute-done | bytes 196640 | tf_op jit(solution)/shard_map/ppermute | solution.py:356
  98.5 11.4 %collective-permute-start.13 = (f32[192,256]{1,0:T(8,128)S(1)}, f32[192,256]{1,0:T(8,128)S(1)}, u32[]{:S(2)}, u32[]{:S(2)}) collective-permute-start(f32[192,256]{1,0:T(8,128)S(1)} %add.37.refs_2_), channel_id=1, source_target_pairs={{0,48},{1,15},{2,50},{3,5},{4,52},{5,3},{6,54},{7,9},{8,56},{9,7},... | collective-permute-start | bytes 589832 | tf_op jit(solution)/shard_map/ppermute | solution.py:356
  109.9 3.1 %collective-permute-done.13.refs_3_ = f32[192,256]{1,0:T(8,128)S(1)} collective-permute-done((f32[192,256]{1,0:T(8,128)S(1)}, f32[192,256]{1,0:T(8,128)S(1)}, u32[]{:S(2)}, u32[]{:S(2)}) %collective-permute-start.13) | collective-permute-done | bytes 196640 | tf_op jit(solution)/shard_map/ppermute | solution.py:356
  113.1 4.4 %shard_map.114.refs_0_ = f32[384,384]{1,0:T(8,128)} custom-call(s32[1]{0:T(128)} %bitcast.core_ref, f32[4,384,384]{2,1,0:T(8,128)} %refs_0_.8, f32[1472,384]{1,0:T(8,128)} %get-tuple-element.30.refs_1_.refs_3_.refs_2_.refs_0_, f32[1472,384]{1,0:T(8,128)} %collective-permute-done.2.refs_2_.refs_4_.refs_1_, ...), custom_call_target="tpu_custom_call" | custom-call | flops 679477248 | bytes 12582912 | tf_op jit(solution)/shard_map/pallas_call | solution.py:133
  117.6 2.5 %shard_map.116 = (f32[384,384]{1,0:T(8,128)}, f32[192,384]{1,0:T(8,128)}) custom-call(s32[1]{0:T(128)} %bitcast.core_ref, f32[384,384]{1,0:T(8,128)} %shard_map.114.refs_0_, f32[576,384]{1,0:T(8,128)} %collective-permute-done.5.refs_1_, f32[576,384]{1,0:T(8,128)} %collective-permute-done.6.refs_2_), custom_call_target="tpu_custom_call" | custom-call | flops 33973864 | bytes 2359296 | tf_op jit(solution)/shard_map/pallas_call | solution.py:133
  120.1 12.3 %collective-permute-start.7 = (f32[384,384]{1,0:T(8,128)}, f32[384,384]{1,0:T(8,128)}, u32[]{:S(2)}, u32[]{:S(2)}) collective-permute-start(f32[384,384]{1,0:T(8,128)} %get-tuple-element.37.refs_0_), channel_id=1, source_target_pairs={{0,1},{1,0},{2,3},{3,2},{4,5},{5,4},{6,7},{7,6},{8,9},{9,8},{10,11... | collective-permute-start | bytes 1769480 | tf_op jit(solution)/shard_map/ppermute | solution.py:379
  133.5 3.8 %shard_map.117 = (f32[4,384,384]{2,1,0:T(8,128)}, f32[4,384,384]{2,1,0:T(8,128)}, f32[4,128,384]{2,1,0:T(8,128)}, f32[4,64,384]{2,1,0:T(8,128)}) custom-call(s32[1]{0:T(128)} %bitcast.core_ref, f32[1472,384]{1,0:T(8,128)} %get-tuple-element.30.refs_1_.refs_3_.refs_2_.refs_0_, f32[1472,384]{1,0:T(8,128)} %collective-permute-done.2.refs_2_.refs_4_.refs_1_, ...), custom_call_target="tpu_custom_call" | custom-call | flops 33973864 | bytes 6684672 | tf_op jit(solution)/shard_map/pallas_call | solution.py:133
  137.3 2.3 %shard_map.118 = (f32[4,384,384]{2,1,0:T(8,128)}, f32[4,384,384]{2,1,0:T(8,128)}, f32[4,128,384]{2,1,0:T(8,128)}, f32[4,64,384]{2,1,0:T(8,128)}) custom-call(s32[1]{0:T(128)} %bitcast.core_ref, f32[384,384]{1,0:T(8,128)} %get-tuple-element.37.refs_0_, ...), custom_call_target="tpu_custom_call", output_to_operand_aliasing={{0}: (4, {}), {1}: (5, {}), {2}: (6, {}), {3}: (7, {})} | custom-call | flops 33973864 | bytes 1474560 | tf_op jit(solution)/shard_map/pallas_call | solution.py:133
  140.3 2.3 %shard_map.119 = (f32[128,256]{1,0:T(8,128)}, f32[64,256]{1,0:T(8,128)}) custom-call(s32[1]{0:T(128)} %bitcast.core_ref, f32[128,256]{1,0:T(8,128)} %refs_0_.9, f32[64,256]{1,0:T(8,128)} %bitcast.10, f32[192,256]{1,0:T(8,128)} %copy-done, f32[192,256]{1,0:T(8,128)} %copy-done.1, f32[192,256]{1,0:T(8,128)} %collective-permute-done.14.refs_4_, ...), custom_call_target="tpu_custom_call" | custom-call | flops 33973864 | bytes 1179648 | tf_op jit(solution)/shard_map/pallas_call | solution.py:133
  (34 shorter events, 7.6 us)
Async XLA Ops:
  0.6 21.0 %collective-permute-start = (f32[4,128,384]{2,1,0:T(8,128)}, f32[4,128,384]{2,1,0:T(8,128)}, u32[]{:S(2)}, u32[]{:S(2)}) collective-permute-start(f32[4,128,384]{2,1,0:T(8,128)} %refs_8_.1), channel_id=1, source_target_pairs={{0,1},{1,0},{2,3},{3,2},{4,5},{5,4},{6,7},{7,6},{8,9},{9,8},{10,11... | collective-permute-start | bytes 2359304 | tf_op jit(solution)/shard_map/ppermute | solution.py:379
  3.9 17.7 %collective-permute-start.1 = (f32[4,64,384]{2,1,0:T(8,128)}, f32[4,64,384]{2,1,0:T(8,128)}, u32[]{:S(2)}, u32[]{:S(2)}) collective-permute-start(f32[4,64,384]{2,1,0:T(8,128)} %bitcast.5), channel_id=1, source_target_pairs={{0,1},{1,0},{2,3},{3,2},{4,5},{5,4},{6,7},{7,6},{8,9},{9,8},{10,11... | collective-permute-start | bytes 1179656 | tf_op jit(solution)/shard_map/ppermute | solution.py:379
  26.5 21.9 %collective-permute-start.2 = (f32[1472,384]{1,0:T(8,128)}, f32[1472,384]{1,0:T(8,128)}, u32[]{:S(2)}, u32[]{:S(2)}) collective-permute-start(f32[1472,384]{1,0:T(8,128)} %get-tuple-element.30.refs_1_.refs_3_.refs_2_.refs_0_), channel_id=1, source_target_pairs={{0,1},{1,0},{2,3},{3,2},{4,5},{5,4},{6,7},{7,6},{8,9},{9,8},{10,11... | collective-permute-start | bytes 6782984 | tf_op jit(solution)/shard_map/ppermute | solution.py:379
  26.8 5.4 %collective-permute-start.3 = (f32[384,384]{1,0:T(8,128)}, f32[384,384]{1,0:T(8,128)}, u32[]{:S(2)}, u32[]{:S(2)}) collective-permute-start(f32[384,384]{1,0:T(8,128)} %get-tuple-element.32.refs_1_), channel_id=1, source_target_pairs={{0,1},{1,0},{2,3},{3,2},{4,5},{5,4},{6,7},{7,6},{8,9},{9,8},{10,11... | collective-permute-start | bytes 1769480 | tf_op jit(solution)/shard_map/ppermute | solution.py:379
  51.9 5.1 %collective-permute-start.8 = (f32[192,256]{1,0:T(8,128)}, f32[192,256]{1,0:T(8,128)S(1)}, u32[]{:S(2)}, u32[]{:S(2)}) collective-permute-start(f32[192,256]{1,0:T(8,128)} %get-tuple-element.47), channel_id=1, source_target_pairs={{0,2},{1,17},{2,0},{3,19},{4,6},{5,21},{6,4},{7,23},{8,10},{9,25},... | collective-permute-start | bytes 589832 | tf_op jit(solution)/shard_map/ppermute | solution.py:356
  58.0 5.8 %collective-permute-start.9 = (f32[192,256]{1,0:T(8,128)S(1)}, f32[192,256]{1,0:T(8,128)S(1)}, u32[]{:S(2)}, u32[]{:S(2)}) collective-permute-start(f32[192,256]{1,0:T(8,128)S(1)} %add.30), channel_id=1, source_target_pairs={{0,14},{1,49},{2,4},{3,51},{4,2},{5,53},{6,8},{7,55},{8,6},{9,57},... | collective-permute-start | bytes 589832 | tf_op jit(solution)/shard_map/ppermute | solution.py:356
  58.8 19.7 %collective-permute-start.4 = (f32[384,384]{1,0:T(8,128)}, f32[384,384]{1,0:T(8,128)}, u32[]{:S(2)}, u32[]{:S(2)}) collective-permute-start(f32[384,384]{1,0:T(8,128)} %get-tuple-element.36), channel_id=1, source_target_pairs={{2,0},{3,1},{4,2},{5,3},{6,4},{7,5},{8,6},{9,7},{10,8},{11,9},{12,... | collective-permute-start | bytes 1769480 | tf_op jit(solution)/shard_map/ppermute | solution.py:387
  63.8 7.2 %collective-permute-start.10 = (f32[192,256]{1,0:T(8,128)S(1)}, f32[192,256]{1,0:T(8,128)S(1)}, u32[]{:S(2)}, u32[]{:S(2)}) collective-permute-start(f32[192,256]{1,0:T(8,128)S(1)} %add_select_fusion.3), channel_id=1, source_target_pairs={{0,2},{1,65},{2,0},{3,67},{4,6},{5,69},{6,4},{7,71},{8,10},{9,73},... | collective-permute-start | bytes 589832 | tf_op jit(solution)/shard_map/ppermute | solution.py:356
  71.7 16.4 %collective-permute-start.11 = (f32[192,256]{1,0:T(8,128)}, f32[192,256]{1,0:T(8,128)}, u32[]{:S(2)}, u32[]{:S(2)}) collective-permute-start(f32[192,256]{1,0:T(8,128)} %add_select_fusion.2), channel_id=1, source_target_pairs={{0,14},{1,193},{2,4},{3,195},{4,2},{5,197},{6,8},{7,199},{8,6},{9,... | collective-permute-start | bytes 589832 | tf_op jit(solution)/shard_map/ppermute | solution.py:356
  84.3 33.2 %collective-permute-start.6 = (f32[576,384]{1,0:T(8,128)}, f32[576,384]{1,0:T(8,128)}, u32[]{:S(2)}, u32[]{:S(2)}) collective-permute-start(f32[576,384]{1,0:T(8,128)} %shard_map.115), channel_id=1, source_target_pairs={{1,3},{3,5},{5,7},{7,9},{9,11},{11,13},{13,15},{15,17},{17,19},{19... | collective-permute-start | bytes 2654216 | tf_op jit(solution)/shard_map/ppermute | solution.py:387
  86.5 31.0 %collective-permute-start.5 = (f32[576,384]{1,0:T(8,128)}, f32[576,384]{1,0:T(8,128)}, u32[]{:S(2)}, u32[]{:S(2)}) collective-permute-start(f32[576,384]{1,0:T(8,128)} %shard_map.115), channel_id=1, source_target_pairs={{0,2},{2,4},{4,6},{6,8},{8,10},{10,12},{12,14},{14,16},{16,18},{18... | collective-permute-start | bytes 2654216 | tf_op jit(solution)/shard_map/ppermute | solution.py:387
  89.1 9.4 %collective-permute-start.12 = (f32[192,256]{1,0:T(8,128)S(1)}, f32[192,256]{1,0:T(8,128)S(1)}, u32[]{:S(2)}, u32[]{:S(2)}) collective-permute-start(f32[192,256]{1,0:T(8,128)S(1)} %add_select_fusion.4), channel_id=1, source_target_pairs={{0,16},{1,3},{2,18},{3,1},{4,20},{5,7},{6,22},{7,5},{8,24},{9,11},... | collective-permute-start | bytes 589832 | tf_op jit(solution)/shard_map/ppermute | solution.py:356
  98.5 19.0 %copy-start = (f32[192,256]{1,0:T(8,128)}, f32[192,256]{1,0:T(8,128)S(1)}, u32[]{:S(2)}) copy-start(f32[192,256]{1,0:T(8,128)S(1)} %add.37.refs_2_) | copy-start | bytes 589828
  98.5 14.4 %collective-permute-start.13 = (f32[192,256]{1,0:T(8,128)S(1)}, f32[192,256]{1,0:T(8,128)S(1)}, u32[]{:S(2)}, u32[]{:S(2)}) collective-permute-start(f32[192,256]{1,0:T(8,128)S(1)} %add.37.refs_2_), channel_id=1, source_target_pairs={{0,48},{1,15},{2,50},{3,5},{4,52},{5,3},{6,54},{7,9},{8,56},{9,7},... | collective-permute-start | bytes 589832 | tf_op jit(solution)/shard_map/ppermute | solution.py:356
  112.9 4.6 %copy-start.1 = (f32[192,256]{1,0:T(8,128)}, f32[192,256]{1,0:T(8,128)S(1)}, u32[]{:S(2)}) copy-start(f32[192,256]{1,0:T(8,128)S(1)} %collective-permute-done.13.refs_3_) | copy-start | bytes 589828
  113.0 19.5 %collective-permute-start.14 = (f32[192,256]{1,0:T(8,128)S(1)}, f32[192,256]{1,0:T(8,128)}, u32[]{:S(2)}, u32[]{:S(2)}) collective-permute-start(f32[192,256]{1,0:T(8,128)S(1)} %add_select_fusion.1), channel_id=1, source_target_pairs={{0,64},{1,3},{2,66},{3,1},{4,68},{5,7},{6,70},{7,5},{8,72},{9,11},... | collective-permute-start | bytes 589832 | tf_op jit(solution)/shard_map/ppermute | solution.py:356
  120.1 17.2 %collective-permute-start.7 = (f32[384,384]{1,0:T(8,128)}, f32[384,384]{1,0:T(8,128)}, u32[]{:S(2)}, u32[]{:S(2)}) collective-permute-start(f32[384,384]{1,0:T(8,128)} %get-tuple-element.37.refs_0_), channel_id=1, source_target_pairs={{0,1},{1,0},{2,3},{3,2},{4,5},{5,4},{6,7},{7,6},{8,9},{9,8},{10,11... | collective-permute-start | bytes 1769480 | tf_op jit(solution)/shard_map/ppermute | solution.py:379
  133.4 3.9 %copy-start.2 = (f32[192,256]{1,0:T(8,128)}, f32[192,256]{1,0:T(8,128)S(1)}, u32[]{:S(2)}) copy-start(f32[192,256]{1,0:T(8,128)S(1)} %add_select_fusion.refs_5_) | copy-start | bytes 589828
  133.4 6.2 %collective-permute-start.15 = (f32[192,256]{1,0:T(8,128)S(1)}, f32[192,256]{1,0:T(8,128)S(1)}, u32[]{:S(2)}, u32[]{:S(2)}) collective-permute-start(f32[192,256]{1,0:T(8,128)S(1)} %add_select_fusion.refs_5_), channel_id=1, source_target_pairs={{0,192},{1,15},{2,194},{3,5},{4,196},{5,3},{6,198},{7,9},{8,200},{... | collective-permute-start | bytes 589832 | tf_op jit(solution)/shard_map/ppermute | solution.py:356
  139.7 0.7 copy-start.3

commit v2 on v1

--- a/solution.py
+++ b/solution.py
@@ -259,11 +259,11 @@
 def next_body(core, ins, outs, held, drain):
     ln, y3, y2, x3, v3, z3, x2, vz2 = ins
     lnp_s, lnn_s, a_s, o_s = held
-    out = outs[0]
+    out_d, out_l, out_c = outs
     mine, _ = core_rows(core, HALF)
     lnp_s[...] = -mm(ln.get(), y3.get())
     lnn_s[...] = -mm(lnp_s[mine, :], y2.get())
-    drain.send(lnn_s, out.at[pl.ds(HALF, HALF)])
+    drain.send(lnn_s, out_l)
     a_s[0:HALF, :] = mm(ln.ref()[mine, :], x3.get())
     a_s[HALF : HALF + ROWS, :] = v3.get()
     a_s[HALF + ROWS :, :] = z3.get()
@@ -271,25 +271,23 @@
     a_s[0:HALF, :] = mm(lnp_s[mine, :], x2.get())
     a_s[HALF:, :] = vz2.get()
     o_s[...] = o_s[...] + mm(a_s[...], lnp_s[...], nt=True)
-    drain.send(o_s.at[pl.ds(0, HALF)], out.at[pl.ds(0, HALF)])
-    drain.send(o_s.at[pl.ds(HALF, HALF)], out.at[pl.ds(N, HALF)])
+    drain.send(o_s.at[pl.ds(0, HALF)], out_d)
+    drain.send(o_s.at[pl.ds(HALF, HALF)], out_c)
 
 
 def left_body(core, ins, outs, held, drain):
     l1, y1, v1, z1, lp, y2, vz2, d, c, b = ins
-    t_s, a_s, e_s = held
-    mine, _ = core_rows(core, HALF)
-    t_s[...] = l1.get().T
-    e_s[0:HALF, :] = mm(t_s[mine, :], y1.get())
+    a_s, e_s = held
+    e_s[0:N, :] = mm(l1.get().T, y1.get())
     a_s[0:ROWS, :] = v1.get()
     a_s[ROWS:, :] = z1.get()
-    e_s[HALF:, :] = mm(a_s[...], l1.get())
-    t_s[...] = lp.get().T
-    e_s[0:HALF, :] = d.ref()[mine, :] - (e_s[0:HALF, :] + mm(t_s[mine, :], y2.get()))
-    both = e_s[HALF:, :] + mm(vz2.get(), lp.get())
-    e_s[HALF : HALF + ROWS, :] = c.get() - both[0:ROWS]
-    e_s[HALF + ROWS :, :] = b.get() - both[ROWS:]
-    drain.send(e_s, outs[0])
+    e_s[N:, :] = mm(a_s[...], l1.get())
+    e_s[0:N, :] = d.get() - (e_s[0:N, :] + mm(lp.get().T, y2.get()))
+    drain.send(e_s.at[pl.ds(0, N)], outs[0].at[pl.ds(0, N)])
+    both = e_s[N:, :] + mm(vz2.get(), lp.get())
+    e_s[N : N + ROWS, :] = c.get() - both[0:ROWS]
+    e_s[N + ROWS :, :] = b.get() - both[ROWS:]
+    drain.send(e_s.at[pl.ds(N, HALF)], outs[0].at[pl.ds(N, HALF)])
 
 
 def place_body(core, ins, outs, held, drain):
@@ -300,43 +298,35 @@
     drain.send(vz2.at[pl.ds(ROWS, COLS)], outs[3].at[2])
 
 
-def half_body(core, ins, outs, held, drain):
-    e, n = ins
-    h_s, r_s = held
-    h_s[0:HALF, :] = e.ref()[0:HALF, :] - n.ref()[0:HALF, :]
-    h_s[HALF:, :] = n.ref()[HALF : 2 * HALF, :]
-    drain.send(h_s, outs[0])
-    r_s[...] = e.ref()[HALF:, :] - n.ref()[N:, :]
-    drain.send(r_s, outs[1])
-
-
 def final_body(core, ins, outs, held, drain):
-    top, right, s6, q6, q7, s8, q8 = ins
-    sum_s, block_s, right_s = held
-    a = s6.get() + q8.get()
-    sum_s[...] = jnp.where(core == 0, s8.get() + q8.get(), a + (q6.get() + q7.get()))
-    block_s[...] = top.get() - sum_s[0:ROWS]
+    top, right, value, other = ins
+    block_s, right_s = held
+    total = value.get() + other.get()
+    block_s[...] = top.get() - total[0:ROWS]
     drain.send(block_s, outs[0])
-    right_s[...] = right.get() - sum_s[ROWS:]
+    right_s[...] = right.get() - total[ROWS:]
     drain.send(right_s, outs[1])
 
 
 def kept_body(core, ins, outs, held, drain):
-    h, hx, rest = ins
+    edge, near_d, far_d, near_l, far_l, near_c = ins
+    d_s, c_s = held
     mine, other = core_rows(core, HALF)
-    for half, where in ((h, mine), (hx, other)):
-        ref = half.ref()
-        drain.send(ref.at[pl.ds(0, HALF)], outs[0].at[0, where])
-        drain.send(ref.at[pl.ds(HALF, HALF)], outs[1].at[0, where])
-    ref = rest.ref()
-    drain.send(ref.at[pl.ds(0, ROWS)], outs[2].at[0])
-    drain.send(ref.at[pl.ds(ROWS, COLS)], outs[3].at[0])
+    e = edge.ref()
+    drain.send(near_l.ref(), outs[1].at[0, mine])
+    drain.send(far_l.ref(), outs[1].at[0, other])
+    d_s[mine, :] = e[mine, :] - near_d.get()
+    d_s[other, :] = e[other, :] - far_d.get()
+    drain.send(d_s, outs[0].at[0])
+    c_s[...] = e[N:, :] - near_c.get()
+    drain.send(c_s.at[pl.ds(0, ROWS)], outs[2].at[0])
+    drain.send(c_s.at[pl.ds(ROWS, COLS)], outs[3].at[0])
 
 
 RINGS = {"y": (4, 32), "x": (4, 8), "z": (8, 1)}
 ORDERS = (
     (("z", 0), ("z", 1), ("z", 0), ("z", 1), ("x", 0), ("x", 1), ("y", 0), ("y", 1)),
-    (("x", 0), ("x", 1), ("y", 0), ("y", 1), ("z", 0), ("z", 1), ("z", 0), ("z", 1)),
+    (("z", 0), ("z", 1), ("z", 0), ("z", 1), ("y", 0), ("y", 1), ("x", 0), ("x", 1)),
 )
 
 
@@ -356,40 +346,29 @@
     return lax.ppermute(value, ("tm", "rhs"), route)
 
 
-def sum_over_tm(v, first):
-    q1 = step(v, 0)
-    a = v + q1
-    q2 = step(a, 1)
-    s3 = jnp.where(first, q2, a + q2)
-    q3 = step(s3, 2)
-    s4 = jnp.where(first, q3, s3 + q3)
-    q4 = step(s4, 3)
-    s5 = jnp.where(first, (a + q4) + (q2 + q3), s4 + q4)
-    q5 = step(s5, 4)
-    s6 = s5 + q5
-    q6 = step(s6, 5)
-    s7 = jnp.where(first, s6 + q6, q6)
-    q7 = step(s7, 6)
-    s8 = jnp.where(first, s7 + q7, q7)
-    q8 = step(s8, 7)
-    return s6, q6, q7, s8, q8
+def sum_over_tm(v):
+    a = v + step(v, 0)
+    near = step(a, 1)
+    far = step(near, 2)
+    last = step(far, 3)
+    value = (a + last) + (near + far)
+    for number in range(4, 7):
+        value = value + step(value, number)
+    return value, step(value, 7)
 
 
 def swapped(value):
     return lax.ppermute(value, "rhs", [(0, 1), (1, 0)])
 
 
-def along(value, distance, core=None):
+def along(value, distance):
     devices = range(lax.axis_size("tm"))
-    pairs = [(i, i + distance) for i in devices if i + distance in devices]
-    cores = (0, 1) if core is None else (core,)
-    route = [(i * 2 + c, j * 2 + c) for i, j in pairs for c in cores]
-    return lax.ppermute(value, ("tm", "rhs"), route)
+    route = [(i, i + distance) for i in devices if i + distance in devices]
+    return lax.ppermute(value, "tm", route)
 
 
 def per_device(diag, link, arrow, right, arrow_block, arrow_rhs):
     core = lax.axis_index("rhs")
-    first = core == 0
     me = jnp.reshape(core, (1,)).astype(jnp.int32)
     square = (N, N)
     right = jnp.swapaxes(right, 1, 2)
@@ -431,7 +410,7 @@
         ],
         [(HALF, N), (HALF, 256)], scratch=[(256, N), (HALF, N), (HALF, 256)], units=2,
     )
-    pieces = sum_over_tm(sums, first)
+    pieces = sum_over_tm(sums)
 
     x_1 = (square, [(snd, rows(0, N)), (rcv, rows(0, N))])
     x_3 = (square, [(rcv, rows(0, N)), (snd, rows(0, N))])
@@ -450,39 +429,39 @@
     )
     l_p = (square, [(link_p, whole)])
     y_2 = (square, [(y2, whole)])
-    (ahead,) = call(
+    ahead_d, ahead_l, ahead_c = call(
         next_body, me, [l_n, y_3, y_2, x_3, v_3, z_3, x_2, vz_2],
-        [(576, N)], scratch=[square, (HALF, N), square, square], room=ROOM, units=4.5,
-    )
-    behind1 = along(ahead, 1, 1)
-    behind0 = along(ahead, 1, 0)
+        [(HALF, N)] * 3, scratch=[square, (HALF, N), square, square], room=ROOM, units=4.5,
+    )
+    behind_d = along(ahead_d, 1)
+    behind_l = along(ahead_l, 1)
+    behind_c = along(ahead_c, 1)
+    far_d = swapped(behind_d)
+    far_l = swapped(behind_l)
     (edge,) = call(
         left_body, me,
         [
             (square, [(link, at(1))]), y_1, v_1, z_1, l_p, y_2, vz_2,
             (square, [(diag, at(0))]), (strip, [(arrow, at(0))]), (slim, [(right, at(0))]),
         ],
-        [square], scratch=[square, (HALF, N), square], room=ROOM, units=2,
+        [(576, N)], scratch=[(HALF, N), (576, N)], room=ROOM, units=3,
     )
     placed = call(
         place_body, me, [x_1, x_3, x_2, y_1, y_3, y_2, v_1, v_3, z_1, z_3, vz_2],
         [(4, N, N), (4, N, N), (4, ROWS, N), (4, COLS, N)], room=ROOM, units=0.1,
     )
-    halves, rest = call(
-        half_body, me, [(square, [(edge, whole)]), ((576, N), [(behind0, whole), (behind1, whole)])],
-        [square, (HALF, N)], scratch=[square, (HALF, N)], room=ROOM, units=0.1,
-    )
-    halves_x = swapped(halves)
     outs = call(
         kept_body, me,
-        [(square, [(halves, whole)]), (square, [(halves_x, whole)]), ((HALF, N), [(rest, whole)])],
-        [(4, N, N), (4, N, N), (4, ROWS, N), (4, COLS, N)], room=ROOM, units=0.1, alias=placed,
+        [((576, N), [(edge, whole)])]
+        + [((HALF, N), [(part, whole)]) for part in (behind_d, far_d, behind_l, far_l, behind_c)],
+        [(4, N, N), (4, N, N), (4, ROWS, N), (4, COLS, N)], scratch=[square, (HALF, N)], room=ROOM, units=0.1,
+        alias=placed,
     )
     reduced, reduced_right = call(
         final_body, me,
         [((ROWS, 256), [(arrow_block, whole)]), ((COLS, 256), [(jnp.swapaxes(arrow_rhs, 0, 1), whole)])]
         + [((HALF, 256), [(piece, whole)]) for piece in pieces],
-        [(ROWS, 256), (COLS, 256)], scratch=[(HALF, 256), (ROWS, 256), (COLS, 256)], room=ROOM, units=0.1,
+        [(ROWS, 256), (COLS, 256)], scratch=[(ROWS, 256), (COLS, 256)], room=ROOM, units=0.1,
     )
     return outs[0], outs[1], outs[2], jnp.swapaxes(outs[3], 1, 2), reduced, jnp.swapaxes(reduced_right, 0, 1)
 

time: 143 us -> 146 us (1.021)
  the two profiles are of different devices: /device:TPU:1 before, /device:TPU:8 now
where the time goes in v2:
time: 146 us
  Pallas kernels  64.6 us (44%)
  waiting for transfers between devices  48.1 us (33%)
  starting transfers between devices  30.2 us (21%)
  other arithmetic  2.01 us (1%)
    pallas_call x10, Pallas kernels, call(): pl.pallas_call(kernel, out_shape=[jax.ShapeDtypeStruct(shape, F32) for sh...  64.6 us
    ppermute x8, waiting for transfers between devices, step(): return lax.ppermute(value, ('tm', 'rhs'), route)  43 us
    ppermute x8, starting transfers between devices, step(): return lax.ppermute(value, ('tm', 'rhs'), route)  14.8 us
    ppermute x4, starting transfers between devices, along(): return lax.ppermute(value, 'tm', route)  13.6 us
    ppermute x6, waiting for transfers between devices, swapped(): return lax.ppermute(value, 'rhs', [(0, 1), (1, 0)])  5.08 us
  transfers between devices with their start and end apart: 18, of which 7 were waited for; matrix products, arithmetic and copies ran while one was open for 1% of the time, Pallas kernels for 37%

profile of v2, /device:TPU:8, one launch (start us, length us, event | category | flops | bytes accessed | tf_op | source)
XLA Modules:
  0.0 145.9 jit_solution(9831632070117988691)
XLA Ops:
  1.2 17.4 %shard_map.109 = (f32[384,384]{1,0:T(8,128)}, f32[384,384]{1,0:T(8,128)}, f32[384,384]{1,0:T(8,128)}, f32[384,384]{1,0:T(8,128)}) custom-call(s32[1]{0:T(128)} %bitcast.core_ref, f32[4,384,384]{2,1,0:T(8,128)} %refs_7_.1, f32[4,384,384]{2,1,0:T(8,128)} %refs_0_.8), custom_call_target="tpu_custom_call" | custom-call | flops 8153726976 | bytes 4718592 | tf_op jit(solution)/shard_map/pallas_call | solution.py:133
  18.7 4.8 %shard_map.110 = (f32[1472,384]{1,0:T(8,128)}, f32[448,384]{1,0:T(8,128)}) custom-call(s32[1]{0:T(128)} %bitcast.core_ref, f32[384,384]{1,0:T(8,128)} %get-tuple-element.29.refs_0_, f32[4,128,384]{2,1,0:T(8,128)} %refs_8_.1, f32[4,128,384]{2,1,0:T(8,128)} %collective-permute-done.refs_2_, f32[4,64,384]{2,1,0:T(8,128)} %bitcast.6, ...), custom_call_target="tpu_custom_call" | custom-call | flops 1358954496 | bytes 5898240 | tf_op jit(solution)/shard_map/pallas_call | solution.py:133
  24.1 5.1 %collective-permute-done.3.refs_2_ = f32[384,384]{1,0:T(8,128)} collective-permute-done((f32[384,384]{1,0:T(8,128)}, f32[384,384]{1,0:T(8,128)}, u32[]{:S(2)}, u32[]{:S(2)}) %collective-permute-start.3) | collective-permute-done | bytes 589856 | tf_op jit(solution)/shard_map/ppermute | solution.py:361
  29.2 16.2 %shard_map.111.refs_3_.refs_0_.refs_5_.refs_2_ = f32[384,384]{1,0:T(8,128)} custom-call(s32[1]{0:T(128)} %bitcast.core_ref, f32[4,384,384]{2,1,0:T(8,128)} %refs_7_.1, f32[384,384]{1,0:T(8,128)} %get-tuple-element.33.refs_1_, f32[384,384]{1,0:T(8,128)} %collective-permute-done.3.refs_2_), custom_call_target="tpu_custom_call" | custom-call | flops 7474249728 | bytes 3538944 | tf_op jit(solution)/shard_map/pallas_call | solution.py:133
  45.4 3.5 %shard_map.113 = (f32[192,384]{1,0:T(8,128)}, f32[192,256]{1,0:T(8,128)}) custom-call(s32[1]{0:T(128)} %bitcast.core_ref, f32[384,384]{1,0:T(8,128)} %shard_map.111.refs_3_.refs_0_.refs_5_.refs_2_, f32[4,128,384]{2,1,0:T(8,128)} %refs_8_.1, f32[4,128,384]{2,1,0:T(8,128)} %collective-permute-done.refs_2_, ...), custom_call_target="tpu_custom_call" | custom-call | flops 679477248 | bytes 7766016 | tf_op jit(solution)/shard_map/pallas_call | solution.py:133
  48.9 2.0 %collective-permute-start.10 = (f32[192,256]{1,0:T(8,128)}, f32[192,256]{1,0:T(8,128)S(1)}, u32[]{:S(2)}, u32[]{:S(2)}) collective-permute-start(f32[192,256]{1,0:T(8,128)} %get-tuple-element.49), channel_id=1, source_target_pairs={{0,2},{1,3},{2,0},{3,1},{4,6},{5,7},{6,4},{7,5},{8,10},{9,11},{10,... | collective-permute-start | bytes 589832 | tf_op jit(solution)/shard_map/ppermute | solution.py:346
  50.9 5.6 %collective-permute-done.10 = f32[192,256]{1,0:T(8,128)S(1)} collective-permute-done((f32[192,256]{1,0:T(8,128)}, f32[192,256]{1,0:T(8,128)S(1)}, u32[]{:S(2)}, u32[]{:S(2)}) %collective-permute-start.10) | collective-permute-done | bytes 196640 | tf_op jit(solution)/shard_map/ppermute | solution.py:346
  57.4 5.8 %collective-permute-start.11 = (f32[192,256]{1,0:T(8,128)S(1)}, f32[192,256]{1,0:T(8,128)S(1)}, u32[]{:S(2)}, u32[]{:S(2)}) collective-permute-start(f32[192,256]{1,0:T(8,128)S(1)} %add.21), channel_id=1, source_target_pairs={{0,14},{1,15},{2,4},{3,5},{4,2},{5,3},{6,8},{7,9},{8,6},{9,7},{10,... | collective-permute-start | bytes 589832 | tf_op jit(solution)/shard_map/ppermute | solution.py:346
  63.2 4.5 %collective-permute-done.11 = f32[192,256]{1,0:T(8,128)S(1)} collective-permute-done((f32[192,256]{1,0:T(8,128)S(1)}, f32[192,256]{1,0:T(8,128)S(1)}, u32[]{:S(2)}, u32[]{:S(2)}) %collective-permute-start.11) | collective-permute-done | bytes 196640 | tf_op jit(solution)/shard_map/ppermute | solution.py:346
  67.7 6.9 %collective-permute-start.4 = (f32[384,384]{1,0:T(8,128)}, f32[384,384]{1,0:T(8,128)}, u32[]{:S(2)}, u32[]{:S(2)}) collective-permute-start(f32[384,384]{1,0:T(8,128)} %get-tuple-element.37), channel_id=1, source_target_pairs={{2,0},{4,2},{6,4},{8,6},{10,8},{12,10},{14,12},{16,14},{18,16},{20... | collective-permute-start | bytes 1769480 | tf_op jit(solution)/shard_map/ppermute | solution.py:367
  76.4 14.1 %collective-permute-done.13 = f32[192,256]{1,0:T(8,128)S(1)} collective-permute-done((f32[192,256]{1,0:T(8,128)S(1)}, f32[192,256]{1,0:T(8,128)S(1)}, u32[]{:S(2)}, u32[]{:S(2)}) %collective-permute-start.13) | collective-permute-done | bytes 196640 | tf_op jit(solution)/shard_map/ppermute | solution.py:346
  90.8 3.6 %shard_map.112 = (f32[384,384]{1,0:T(8,128)}, f32[384,384]{1,0:T(8,128)}) custom-call(s32[1]{0:T(128)} %bitcast.core_ref, f32[4,384,384]{2,1,0:T(8,128)} %refs_0_.8, f32[1472,384]{1,0:T(8,128)} %get-tuple-element.31.refs_1_.refs_3_.refs_2_.refs_0_, f32[1472,384]{1,0:T(8,128)} %collective-permute-done.2.refs_2_.refs_4_.refs_1_, ...), custom_call_target="tpu_custom_call" | custom-call | flops 679477248 | bytes 7471104 | tf_op jit(solution)/shard_map/pallas_call | solution.py:133
  94.4 5.8 %shard_map.115 = (f32[192,384]{1,0:T(8,128)}, f32[192,384]{1,0:T(8,128)}, f32[192,384]{1,0:T(8,128)}) custom-call(s32[1]{0:T(128)} %bitcast.core_ref, f32[384,384]{1,0:T(8,128)} %collective-permute-done.4.refs_0_, f32[1472,384]{1,0:T(8,128)} %collective-permute-done.2.refs_2_.refs_4_.refs_1_, f32[1472,384]{1,0:T(8,128)} %get-tuple-element.31.refs_1_.refs_3_.refs_2_.refs_0_, ...), custom_call_target="tpu_custom_call" | custom-call | flops 1528823808 | bytes 7274496 | tf_op jit(solution)/shard_map/pallas_call | solution.py:133
  100.1 2.8 %collective-permute-start.5 = (f32[192,384]{1,0:T(8,128)}, f32[192,384]{1,0:T(8,128)S(1)}, u32[]{:S(2)}, u32[]{:S(2)}) collective-permute-start(f32[192,384]{1,0:T(8,128)} %get-tuple-element.38), channel_id=1, source_target_pairs={{0,2},{2,4},{4,6},{6,8},{8,10},{10,12},{12,14},{14,16},{16,18},{18... | collective-permute-start | bytes 884744 | tf_op jit(solution)/shard_map/ppermute | solution.py:367
  103.0 1.9 %collective-permute-start.7 = (f32[192,384]{1,0:T(8,128)}, f32[192,384]{1,0:T(8,128)}, u32[]{:S(2)}, u32[]{:S(2)}) collective-permute-start(f32[192,384]{1,0:T(8,128)} %get-tuple-element.39), channel_id=1, source_target_pairs={{0,2},{2,4},{4,6},{6,8},{8,10},{10,12},{12,14},{14,16},{16,18},{18... | collective-permute-start | bytes 884744 | tf_op jit(solution)/shard_map/ppermute | solution.py:367
  105.9 2.2 %collective-permute-start.15 = (f32[192,256]{1,0:T(8,128)S(1)}, f32[192,256]{1,0:T(8,128)S(1)}, u32[]{:S(2)}, u32[]{:S(2)}) collective-permute-start(f32[192,256]{1,0:T(8,128)S(1)} %add.25), channel_id=1, source_target_pairs={{0,48},{1,193},{2,50},{3,195},{4,52},{5,197},{6,54},{7,199},{8,56}... | collective-permute-start | bytes 589832 | tf_op jit(solution)/shard_map/ppermute | solution.py:346
  108.0 14.9 %collective-permute-done.15 = f32[192,256]{1,0:T(8,128)S(1)} collective-permute-done((f32[192,256]{1,0:T(8,128)S(1)}, f32[192,256]{1,0:T(8,128)S(1)}, u32[]{:S(2)}, u32[]{:S(2)}) %collective-permute-start.15) | collective-permute-done | bytes 196640 | tf_op jit(solution)/shard_map/ppermute | solution.py:346
  123.1 1.9 %collective-permute-start.9 = (f32[192,384]{1,0:T(8,128)}, f32[192,384]{1,0:T(8,128)}, u32[]{:S(2)}, u32[]{:S(2)}) collective-permute-start(f32[192,384]{1,0:T(8,128)} %get-tuple-element.40), channel_id=1, source_target_pairs={{0,2},{2,4},{4,6},{6,8},{8,10},{10,12},{12,14},{14,16},{16,18},{18... | collective-permute-start | bytes 884744 | tf_op jit(solution)/shard_map/ppermute | solution.py:367
  125.6 3.1 %collective-permute-done.16 = f32[192,256]{1,0:T(8,128)S(1)} collective-permute-done((f32[192,256]{1,0:T(8,128)S(1)}, f32[192,256]{1,0:T(8,128)S(1)}, u32[]{:S(2)}, u32[]{:S(2)}) %collective-permute-start.16) | collective-permute-done | bytes 196640 | tf_op jit(solution)/shard_map/ppermute | solution.py:346
  128.8 3.7 %collective-permute-start.17 = (f32[192,256]{1,0:T(8,128)S(1)}, f32[192,256]{1,0:T(8,128)}, u32[]{:S(2)}, u32[]{:S(2)}) collective-permute-start(f32[192,256]{1,0:T(8,128)S(1)} %add.27.refs_2_), channel_id=1, source_target_pairs={{0,192},{1,49},{2,194},{3,51},{4,196},{5,53},{6,198},{7,55},{8,200... | collective-permute-start | bytes 589832 | tf_op jit(solution)/shard_map/ppermute | solution.py:346
  132.4 3.8 %shard_map.116 = (f32[4,384,384]{2,1,0:T(8,128)}, f32[4,384,384]{2,1,0:T(8,128)}, f32[4,128,384]{2,1,0:T(8,128)}, f32[4,64,384]{2,1,0:T(8,128)}) custom-call(s32[1]{0:T(128)} %bitcast.core_ref, f32[1472,384]{1,0:T(8,128)} %get-tuple-element.31.refs_1_.refs_3_.refs_2_.refs_0_, f32[1472,384]{1,0:T(8,128)} %collective-permute-done.2.refs_2_.refs_4_.refs_1_, ...), custom_call_target="tpu_custom_call" | custom-call | flops 33973864 | bytes 6684672 | tf_op jit(solution)/shard_map/pallas_call | solution.py:133
  136.2 4.8 %shard_map.114.refs_0_ = f32[576,384]{1,0:T(8,128)} custom-call(s32[1]{0:T(128)} %bitcast.core_ref, f32[4,384,384]{2,1,0:T(8,128)} %refs_0_.8, f32[1472,384]{1,0:T(8,128)} %get-tuple-element.31.refs_1_.refs_3_.refs_2_.refs_0_, f32[1472,384]{1,0:T(8,128)} %collective-permute-done.2.refs_2_.refs_4_.refs_1_, ...), custom_call_target="tpu_custom_call" | custom-call | flops 1019215872 | bytes 12582912 | tf_op jit(solution)/shard_map/pallas_call | solution.py:133
  141.1 2.7 %shard_map.117 = (f32[4,384,384]{2,1,0:T(8,128)}, f32[4,384,384]{2,1,0:T(8,128)}, f32[4,128,384]{2,1,0:T(8,128)}, f32[4,64,384]{2,1,0:T(8,128)}) custom-call(s32[1]{0:T(128)} %bitcast.core_ref, f32[576,384]{1,0:T(8,128)} %shard_map.114.refs_0_, f32[192,384]{1,0:T(8,128)} %copy-done.1, ...), custom_call_target="tpu_custom_call", output_to_operand_aliasing={{0}: (7, {}), {1}: (8, {}), {2}: (9, {}), {3}: (10, {})} | custom-call | flops 33973864 | bytes 2359296 | tf_op jit(solution)/shard_map/pallas_call | solution.py:133
  143.8 2.0 %shard_map.118 = (f32[128,256]{1,0:T(8,128)}, f32[64,256]{1,0:T(8,128)}) custom-call(s32[1]{0:T(128)} %bitcast.core_ref, f32[128,256]{1,0:T(8,128)} %refs_0_.9, f32[64,256]{1,0:T(8,128)} %bitcast.10, f32[192,256]{1,0:T(8,128)} %copy-done, f32[192,256]{1,0:T(8,128)} %collective-permute-done.17.refs_3_), custom_call_target="tpu_custom_call" | custom-call | flops 33973864 | bytes 589824 | tf_op jit(solution)/shard_map/pallas_call | solution.py:133
  (31 shorter events, 5.9 us)
Async XLA Ops:
  0.6 18.0 %collective-permute-start = (f32[4,128,384]{2,1,0:T(8,128)}, f32[4,128,384]{2,1,0:T(8,128)}, u32[]{:S(2)}, u32[]{:S(2)}) collective-permute-start(f32[4,128,384]{2,1,0:T(8,128)} %refs_8_.1), channel_id=1, source_target_pairs={{0,1},{1,0},{2,3},{3,2},{4,5},{5,4},{6,7},{7,6},{8,9},{9,8},{10,11... | collective-permute-start | bytes 2359304 | tf_op jit(solution)/shard_map/ppermute | solution.py:361
  0.7 17.9 %collective-permute-start.1 = (f32[4,64,384]{2,1,0:T(8,128)}, f32[4,64,384]{2,1,0:T(8,128)}, u32[]{:S(2)}, u32[]{:S(2)}) collective-permute-start(f32[4,64,384]{2,1,0:T(8,128)} %bitcast.5), channel_id=1, source_target_pairs={{0,1},{1,0},{2,3},{3,2},{4,5},{5,4},{6,7},{7,6},{8,9},{9,8},{10,11... | collective-permute-start | bytes 1179656 | tf_op jit(solution)/shard_map/ppermute | solution.py:361
  23.5 21.9 %collective-permute-start.2 = (f32[1472,384]{1,0:T(8,128)}, f32[1472,384]{1,0:T(8,128)}, u32[]{:S(2)}, u32[]{:S(2)}) collective-permute-start(f32[1472,384]{1,0:T(8,128)} %get-tuple-element.31.refs_1_.refs_3_.refs_2_.refs_0_), channel_id=1, source_target_pairs={{0,1},{1,0},{2,3},{3,2},{4,5},{5,4},{6,7},{7,6},{8,9},{9,8},{10,11... | collective-permute-start | bytes 6782984 | tf_op jit(solution)/shard_map/ppermute | solution.py:361
  23.9 5.3 %collective-permute-start.3 = (f32[384,384]{1,0:T(8,128)}, f32[384,384]{1,0:T(8,128)}, u32[]{:S(2)}, u32[]{:S(2)}) collective-permute-start(f32[384,384]{1,0:T(8,128)} %get-tuple-element.33.refs_1_), channel_id=1, source_target_pairs={{0,1},{1,0},{2,3},{3,2},{4,5},{5,4},{6,7},{7,6},{8,9},{9,8},{10,11... | collective-permute-start | bytes 1769480 | tf_op jit(solution)/shard_map/ppermute | solution.py:361
  48.9 7.6 %collective-permute-start.10 = (f32[192,256]{1,0:T(8,128)}, f32[192,256]{1,0:T(8,128)S(1)}, u32[]{:S(2)}, u32[]{:S(2)}) collective-permute-start(f32[192,256]{1,0:T(8,128)} %get-tuple-element.49), channel_id=1, source_target_pairs={{0,2},{1,3},{2,0},{3,1},{4,6},{5,7},{6,4},{7,5},{8,10},{9,11},{10,... | collective-permute-start | bytes 589832 | tf_op jit(solution)/shard_map/ppermute | solution.py:346
  57.4 10.3 %collective-permute-start.11 = (f32[192,256]{1,0:T(8,128)S(1)}, f32[192,256]{1,0:T(8,128)S(1)}, u32[]{:S(2)}, u32[]{:S(2)}) collective-permute-start(f32[192,256]{1,0:T(8,128)S(1)} %add.21), channel_id=1, source_target_pairs={{0,14},{1,15},{2,4},{3,5},{4,2},{5,3},{6,8},{7,9},{8,6},{9,7},{10,... | collective-permute-start | bytes 589832 | tf_op jit(solution)/shard_map/ppermute | solution.py:346
  67.7 7.8 %collective-permute-start.12 = (f32[192,256]{1,0:T(8,128)S(1)}, f32[192,256]{1,0:T(8,128)S(1)}, u32[]{:S(2)}, u32[]{:S(2)}) collective-permute-start(f32[192,256]{1,0:T(8,128)S(1)} %collective-permute-done.11), channel_id=1, source_target_pairs={{0,2},{1,3},{2,0},{3,1},{4,6},{5,7},{6,4},{7,5},{8,10},{9,11},{10,... | collective-permute-start | bytes 589832 | tf_op jit(solution)/shard_map/ppermute | solution.py:346
  67.7 26.6 %collective-permute-start.4 = (f32[384,384]{1,0:T(8,128)}, f32[384,384]{1,0:T(8,128)}, u32[]{:S(2)}, u32[]{:S(2)}) collective-permute-start(f32[384,384]{1,0:T(8,128)} %get-tuple-element.37), channel_id=1, source_target_pairs={{2,0},{4,2},{6,4},{8,6},{10,8},{12,10},{14,12},{16,14},{18,16},{20... | collective-permute-start | bytes 1769480 | tf_op jit(solution)/shard_map/ppermute | solution.py:367
  75.5 14.9 %collective-permute-start.13 = (f32[192,256]{1,0:T(8,128)S(1)}, f32[192,256]{1,0:T(8,128)S(1)}, u32[]{:S(2)}, u32[]{:S(2)}) collective-permute-start(f32[192,256]{1,0:T(8,128)S(1)} %collective-permute-done.12), channel_id=1, source_target_pairs={{0,14},{1,15},{2,4},{3,5},{4,2},{5,3},{6,8},{7,9},{8,6},{9,7},{10,... | collective-permute-start | bytes 589832 | tf_op jit(solution)/shard_map/ppermute | solution.py:346
  90.5 14.4 %collective-permute-start.14 = (f32[192,256]{1,0:T(8,128)S(1)}, f32[192,256]{1,0:T(8,128)}, u32[]{:S(2)}, u32[]{:S(2)}) collective-permute-start(f32[192,256]{1,0:T(8,128)S(1)} %add_add_fusion), channel_id=1, source_target_pairs={{0,16},{1,65},{2,18},{3,67},{4,20},{5,69},{6,22},{7,71},{8,24},{9,... | collective-permute-start | bytes 589832 | tf_op jit(solution)/shard_map/ppermute | solution.py:346
  100.1 24.9 %collective-permute-start.5 = (f32[192,384]{1,0:T(8,128)}, f32[192,384]{1,0:T(8,128)S(1)}, u32[]{:S(2)}, u32[]{:S(2)}) collective-permute-start(f32[192,384]{1,0:T(8,128)} %get-tuple-element.38), channel_id=1, source_target_pairs={{0,2},{2,4},{4,6},{6,8},{8,10},{10,12},{12,14},{14,16},{16,18},{18... | collective-permute-start | bytes 884744 | tf_op jit(solution)/shard_map/ppermute | solution.py:367
  103.0 22.1 %collective-permute-start.7 = (f32[192,384]{1,0:T(8,128)}, f32[192,384]{1,0:T(8,128)}, u32[]{:S(2)}, u32[]{:S(2)}) collective-permute-start(f32[192,384]{1,0:T(8,128)} %get-tuple-element.39), channel_id=1, source_target_pairs={{0,2},{2,4},{4,6},{6,8},{8,10},{10,12},{12,14},{14,16},{16,18},{18... | collective-permute-start | bytes 884744 | tf_op jit(solution)/shard_map/ppermute | solution.py:367
  105.9 17.1 %collective-permute-start.15 = (f32[192,256]{1,0:T(8,128)S(1)}, f32[192,256]{1,0:T(8,128)S(1)}, u32[]{:S(2)}, u32[]{:S(2)}) collective-permute-start(f32[192,256]{1,0:T(8,128)S(1)} %add.25), channel_id=1, source_target_pairs={{0,48},{1,193},{2,50},{3,195},{4,52},{5,197},{6,54},{7,199},{8,56}... | collective-permute-start | bytes 589832 | tf_op jit(solution)/shard_map/ppermute | solution.py:346
  123.0 5.8 %collective-permute-start.16 = (f32[192,256]{1,0:T(8,128)S(1)}, f32[192,256]{1,0:T(8,128)S(1)}, u32[]{:S(2)}, u32[]{:S(2)}) collective-permute-start(f32[192,256]{1,0:T(8,128)S(1)} %add.26), channel_id=1, source_target_pairs={{0,64},{1,17},{2,66},{3,19},{4,68},{5,21},{6,70},{7,23},{8,72},{9,... | collective-permute-start | bytes 589832 | tf_op jit(solution)/shard_map/ppermute | solution.py:346
  123.1 18.0 %collective-permute-start.9 = (f32[192,384]{1,0:T(8,128)}, f32[192,384]{1,0:T(8,128)}, u32[]{:S(2)}, u32[]{:S(2)}) collective-permute-start(f32[192,384]{1,0:T(8,128)} %get-tuple-element.40), channel_id=1, source_target_pairs={{0,2},{2,4},{4,6},{6,8},{8,10},{10,12},{12,14},{14,16},{16,18},{18... | collective-permute-start | bytes 884744 | tf_op jit(solution)/shard_map/ppermute | solution.py:367
  125.0 11.2 %copy-start.1 = (f32[192,384]{1,0:T(8,128)}, f32[192,384]{1,0:T(8,128)S(1)}, u32[]{:S(2)}) copy-start(f32[192,384]{1,0:T(8,128)S(1)} %collective-permute-done.5.refs_1_) | copy-start | bytes 884740
  125.0 16.0 %collective-permute-start.6 = (f32[192,384]{1,0:T(8,128)S(1)}, f32[192,384]{1,0:T(8,128)}, u32[]{:S(2)}, u32[]{:S(2)}) collective-permute-start(f32[192,384]{1,0:T(8,128)S(1)} %collective-permute-done.5.refs_1_), channel_id=1, source_target_pairs={{0,1},{1,0},{2,3},{3,2},{4,5},{5,4},{6,7},{7,6},{8,9},{9,8},{10,11... | collective-permute-start | bytes 884744 | tf_op jit(solution)/shard_map/ppermute | solution.py:361
  125.1 15.9 %collective-permute-start.8 = (f32[192,384]{1,0:T(8,128)}, f32[192,384]{1,0:T(8,128)}, u32[]{:S(2)}, u32[]{:S(2)}) collective-permute-start(f32[192,384]{1,0:T(8,128)} %collective-permute-done.7.refs_3_), channel_id=1, source_target_pairs={{0,1},{1,0},{2,3},{3,2},{4,5},{5,4},{6,7},{7,6},{8,9},{9,8},{10,11... | collective-permute-start | bytes 884744 | tf_op jit(solution)/shard_map/ppermute | solution.py:361
  128.7 7.4 %copy-start = (f32[192,256]{1,0:T(8,128)}, f32[192,256]{1,0:T(8,128)S(1)}, u32[]{:S(2)}) copy-start(f32[192,256]{1,0:T(8,128)S(1)} %add.27.refs_2_) | copy-start | bytes 589828
  128.8 15.0 %collective-permute-start.17 = (f32[192,256]{1,0:T(8,128)S(1)}, f32[192,256]{1,0:T(8,128)}, u32[]{:S(2)}, u32[]{:S(2)}) collective-permute-start(f32[192,256]{1,0:T(8,128)S(1)} %add.27.refs_2_), channel_id=1, source_target_pairs={{0,192},{1,49},{2,194},{3,51},{4,196},{5,53},{6,198},{7,55},{8,200... | collective-permute-start | bytes 589832 | tf_op jit(solution)/shard_map/ppermute | solution.py:346
